TPU v7x, 32 devices: a whole 2x2x4 slice. The times are simulated.
32 devices in a mesh: area: 4 (over y, core), pos: 8 (over z, x).
Axes of the slice: x: 2, y: 2, z: 4, core: 2. Of those that a mesh axis runs over, the one named last changes fastest.
Arguments:
- exit_wave: bfloat16 [128, 2, 128, 128], P(('area', 'pos')), may hold values from -6 to 6
- amplitude: bfloat16 [128, 128, 128], P(('area', 'pos')), may hold values from 0.19921875 to 5
- probe: float32 [2, 128, 128], replicated, may hold values from -4 to 4
- offsets: int32 [128, 2], P(('area', 'pos')), may hold values from 0 to 127
- owner: int32 [128, 1], P(('area', 'pos')), may hold values from 0 to 7; in each aligned block of 4 rows (0 to 3, 4 to 7, ...) at most 2 rows name the same one
Outputs:
- new_wave: bfloat16 [128, 2, 128, 128], P(('area', 'pos'))
- object_field: float32 [2, 512, 1024], P(None, 'area', 'pos')
Inputs may be any that keep to these rules, and one draw needn't show every extreme that they name: owner names the object tile column that holds the position's patch centre; of the 4 positions of one device at most 2 name the same tile.
All inputs are finite; a program needn't handle non-finite values.
Results may differ from a plain program's by a relative error of at most 0.0059.
Values may be sent and summed in bfloat16 or wider, within the bound.
No kernel may reach another device: no remote copies, remote signals or barrier semaphores. Data moves between devices by JAX's collectives and lax.ppermute only.
A program may use at most 64 MiB of HBM per device.

v0:
```python
import functools
import math

import jax
import jax.numpy as jnp
import numpy as np
from jax import lax
from jax.experimental import pallas as pl
from jax.experimental.pallas import tpu as pltpu
from jax.sharding import PartitionSpec as P


F32 = jnp.float32
BF16 = jnp.bfloat16
VMEM = pl.BlockSpec(memory_space=pltpu.VMEM)
SMEM = pl.BlockSpec(memory_space=pltpu.SMEM)


def lanes_of(rows, size):
    return lax.broadcasted_iota(jnp.int32, (rows, size), 1)


def where_is(meta, device, number):
    return tuple(meta[device, 3 * number + part] for part in range(3))


def place(canvas, tile, channel, row, col, data):
    size = data.shape[0]
    turned = pltpu.roll(data, col, 1)
    wraps = lanes_of(size, size) < col
    rows = pl.ds(row, size)
    canvas[tile, channel, rows, :] += jnp.where(wraps, 0.0, turned)
    canvas[tile + 1, channel, rows, :] += jnp.where(wraps, turned, 0.0)


def cut(canvas, tile, channel, row, col, size):
    rows = pl.ds(row, size)
    here = canvas[tile, channel, rows, :]
    after = canvas[tile + 1, channel, rows, :]
    both = jnp.where(lanes_of(size, size) < col, after, here)
    return pltpu.roll(both, lax.rem(size - col, size), 1)


def tile_part(canvas, tile, channel, row, count, size):
    here = canvas[tile, channel, pl.ds(row, count), :]
    after = canvas[tile + 1, channel, pl.ds(row, count), :]
    half = size // 2
    return pltpu.roll(jnp.where(lanes_of(count, size) < half, after, here), half, 1)


def stage_kernel(held, size, offsets, owner, probe, wave, payload):
    probe_re = probe[0]
    probe_im = probe[1]
    for number in range(held):
        wave_re = wave[number, 0].astype(F32)
        wave_im = wave[number, 1].astype(F32)
        for channel, part in (
            (0, probe_re * wave_re + probe_im * wave_im),
            (1, probe_re * wave_im - probe_im * wave_re),
        ):
            first = (2 * number + channel) * size
            payload[first : first + size, :] = part.astype(BF16)
    rows = payload.shape[0] - 2 * held * size
    row_at = lax.broadcasted_iota(jnp.int32, (rows, size), 0)
    col_at = lanes_of(rows, size)
    tail = jnp.zeros((rows, size), jnp.int32)
    for number in range(held):
        for part, value in enumerate((offsets[0, number], offsets[1, number], owner[0, number])):
            tail = jnp.where((row_at == number) & (col_at == part), value, tail)
    payload[2 * held * size :, :] = tail.astype(F32).astype(BF16)


def place_waves(canvas, held, size, waves, numbers, scalars, sem):
    for at, wave in enumerate(waves):
        numbers[at] = wave[2 * held * size :, :].astype(F32).astype(jnp.int32)
    copy = pltpu.make_async_copy(numbers, scalars, sem)
    copy.start()
    copy.wait()
    for at, wave in enumerate(waves):

        def add_one(number, carry, wave=wave, at=at):
            row = scalars[at, number, 0]
            col = scalars[at, number, 1]
            tile = scalars[at, number, 2]
            for channel in (0, 1):
                first = pl.multiple_of((2 * number + channel) * size, size)
                data = wave[pl.ds(first, size), :].astype(F32)
                place(canvas, tile, channel, row, col, data)
            return carry

        lax.fori_loop(0, held, add_one, 0)


def denominators(areas, columns, held, size, meta, probe, denom, canvas):
    area = lax.axis_index("area")
    pos = lax.axis_index("pos")
    power = probe[0] * probe[0] + probe[1] * probe[1]
    canvas[...] = jnp.zeros_like(canvas)

    for shift in (-1, 0, 1):
        other = area + shift

        @pl.when((other >= 0) & (other < areas))
        def _(other=other, shift=shift):
            @pl.loop(0, columns)
            def _(source):
                for number in range(held):
                    row, col, tile = where_is(meta, other * columns + source, number)
                    place(canvas, tile, 0, row + (shift + 1) * size, col, power)

    for number in range(held):
        row, col, tile = where_is(meta, area * columns + pos, number)
        denom[number] = cut(canvas, tile, 0, row + size, col, size)
    denom[held] = tile_part(canvas, pos, 0, size + size // 2, size, size)


def band_kernel(held, size, fresh, whole, *refs):
    waves = refs[:-4] if fresh else refs[:-5]
    canvas, numbers, scalars, sem = refs[-4:]
    if fresh:
        canvas[...] = jnp.zeros_like(canvas)
    elif not whole:
        canvas[...] = refs[-5][...]
    place_waves(canvas, held, size, waves, numbers, scalars, sem)


def late_kernel(areas, columns, held, size, whole, *refs):
    meta = refs[0]
    given, outer, paired, canvas, numbers, scalars, sem, shifted = refs[-8:]
    if not whole:
        canvas[...] = given[...]
    place_waves(canvas, held, size, refs[1:-8], numbers, scalars, sem)
    cut_messages(areas, columns, held, size, meta, canvas, outer, paired, shifted)


def neighbour(area, outer):
    step = 1 - 2 * lax.rem(area, 2)
    return -step if outer else step


def cut_messages(areas, columns, held, size, meta, canvas, outer, paired, shifted):
    area = lax.axis_index("area")
    pos = lax.axis_index("pos")
    half = size // 2
    for side in (0, 1):
        shifted[side, :size] = jnp.zeros((size, size), F32)
        shifted[side, 2 * size :] = jnp.zeros((size, size), F32)
    for out, is_outer in ((outer, True), (paired, False)):
        step = neighbour(area, is_outer)
        above = step < 0
        device = jnp.clip(area + step, 0, areas - 1) * columns + pos
        block = pl.multiple_of(jnp.where(above, 0, size), 8)
        for number in range(held):
            row, col, tile = where_is(meta, device, number)
            for channel in (0, 1):
                shifted[channel, size : 2 * size] = cut(canvas, tile, channel, block, col, size)
                first = jnp.where(above, row, row + size)
                out[2 * number + channel] = shifted[channel, pl.ds(first, size), :].astype(BF16)
        first = pl.multiple_of(jnp.where(above, 0, size + half), 8)
        for channel in (0, 1):
            out[2 * held, channel * half : (channel + 1) * half] = tile_part(
                canvas, pos, channel, first, half, size
            ).astype(BF16)


def own_kernel(columns, held, size, meta, canvas, own):
    pos = lax.axis_index("pos")
    me = lax.axis_index("area") * columns + pos
    for number in range(held):
        row, col, tile = where_is(meta, me, number)
        for channel in (0, 1):
            own[2 * number + channel] = cut(canvas, tile, channel, row, col, size)
    for channel in (0, 1):
        own[2 * held + channel] = tile_part(canvas, pos, channel, size // 2, size, size)


def split(value):
    high = value.astype(BF16)
    return (high, (value - high.astype(F32)).astype(BF16))


def from_right(data, matrix):
    high, low = data
    return jnp.dot(
        jnp.concatenate([high, low, high], 1), matrix, preferred_element_type=F32
    )


def from_left(matrix, data):
    high, low = data
    return jnp.dot(
        matrix, jnp.concatenate([high, low, high], 0), preferred_element_type=F32
    )


def to_columns(value, held, size):
    return jnp.concatenate(
        [
            jnp.concatenate(
                [
                    value[number * size : (number + 1) * size, part * size : (part + 1) * size]
                    for number in range(held)
                ],
                1,
            )
            for part in (0, 1)
        ],
        0,
    )


def final_kernel(areas, columns, held, size, *refs):
    meta, own, outer, paired, denom, wave, amplitude, probe, right, left = refs[:10]
    new_wave, tile_out, rows_high, rows_low, proj = refs[10:]
    area = lax.axis_index("area")
    pos = lax.axis_index("pos")
    half = size // 2
    me = area * columns + pos
    odd = lax.rem(area, 2) == 1
    scale = 1.0 / (denom[held] + 0.1)
    for channel in (0, 1):
        rows = slice(channel * half, (channel + 1) * half)
        sums = own[2 * held + channel]
        one = outer[2 * held, rows].astype(F32)
        two = paired[2 * held, rows].astype(F32)
        sums = sums + jnp.concatenate([jnp.where(odd, two, one), jnp.where(odd, one, two)], 0)
        tile_out[channel] = sums * scale
    probe_re = probe[0]
    probe_im = probe[1]
    row_at = lax.broadcasted_iota(jnp.int32, (size, size), 0)
    col_at = lanes_of(size, size)
    for number in range(held):
        row, col, tile = where_is(meta, me, number)
        top = area * size + row - half
        start = tile * size + col - half
        inside = (
            (row_at >= -top)
            & (row_at < areas * size - top)
            & (col_at >= -start)
            & (col_at < columns * size - start)
        )
        share = jnp.where(inside, 1.0 / (denom[number] + 0.1), 0.0)
        patch = []
        for channel in (0, 1):
            at = 2 * number + channel
            sums = own[at] + (outer[at].astype(F32) + paired[at].astype(F32))
            patch.append((sums * share).astype(BF16).astype(F32))
        proj_re = probe_re * patch[0] - probe_im * patch[1]
        proj_im = probe_re * patch[1] + probe_im * patch[0]
        proj[number, 0] = proj_re
        proj[number, 1] = proj_im
        at = slice(number * size, (number + 1) * size)
        for channel, part in ((0, proj_re), (1, proj_im)):
            high, low = split(2.0 * part - wave[number, channel].astype(F32))
            rows_high[at, channel * size : (channel + 1) * size] = high
            rows_low[at, channel * size : (channel + 1) * size] = low
    mid = to_columns(from_right((rows_high[...], rows_low[...]), right[0]), held, size)
    spectrum = from_left(left[0], split(mid))
    for number in range(held):
        at = slice(number * size, (number + 1) * size)
        spec_re = spectrum[:size, at]
        spec_im = spectrum[size:, at]
        ratio = amplitude[number].astype(F32) * lax.rsqrt(
            spec_re * spec_re + spec_im * spec_im + 0.01
        )
        for channel, part in ((0, spec_re), (1, spec_im)):
            high, low = split(part * ratio)
            rows_high[at, channel * size : (channel + 1) * size] = high
            rows_low[at, channel * size : (channel + 1) * size] = low
    mid = to_columns(from_right((rows_high[...], rows_low[...]), right[1]), held, size)
    back = from_left(left[1], split(mid))
    for number in range(held):
        at = slice(number * size, (number + 1) * size)
        for channel in (0, 1):
            new_wave[number, channel] = (
                0.75 * wave[number, channel].astype(F32)
                - 0.5 * proj[number, channel]
                + 0.75 * back[channel * size : (channel + 1) * size, at]
            ).astype(BF16)


def twiddles(size):
    at = np.arange(size)
    angle = 2.0 * math.pi * ((at[:, None] * at[None, :]) % size) / size
    real = np.cos(angle) / math.sqrt(size)
    imag = -np.sin(angle) / math.sqrt(size)

    def parts(whole, axis):
        whole = whole.astype(np.float32)
        high = whole.astype(BF16)
        low = (whole - high.astype(np.float32)).astype(BF16)
        return np.concatenate([high, high, low], axis)

    right = [parts(np.block([[real, im], [-im, real]]), 0) for im in (imag, -imag)]
    left = [parts(np.block([[real, -im], [im, real]]), 1) for im in (imag, -imag)]
    return (jnp.asarray(np.stack(right)), jnp.asarray(np.stack(left)))


def steps_of(lines):
    return sorted(range(1, lines), key=lambda step: (step != lines // 2, step))


def gathered(wave, columns):
    inner = 2 if columns % 2 == 0 else 1
    lines = columns // inner
    xor = lines & (lines - 1) == 0
    pieces = {(0, False): wave}
    for step in steps_of(lines):
        pairs = [
            (i, (i // inner ^ step if xor else (i // inner + step) % lines) * inner + i % inner)
            for i in range(columns)
        ]
        pieces[step, False] = lax.ppermute(wave, "pos", pairs)
    if inner == 2:
        for step in range(lines):
            pieces[step, True] = lax.ppermute(
                pieces[step, False], "pos", [(i, i ^ 1) for i in range(columns)]
            )
    return pieces


def on_chip(values):
    if sum(value.size * value.dtype.itemsize for value in values) > 2**23:
        return list(values)
    return [pltpu.with_memory_space_constraint(value, pltpu.VMEM) for value in values]


def limit(*values):
    held = sum(math.prod(value.shape) * np.dtype(value.dtype).itemsize for value in values)
    return pltpu.CompilerParams(vmem_limit_bytes=min(held + 2**23, 60 * 2**20))


SMALL = 6 * 2**20


def room(shape, dtype):
    if math.prod(shape) * np.dtype(dtype).itemsize <= SMALL:
        return pltpu.VMEM(shape, dtype)
    return jax.ShapeDtypeStruct(shape, dtype)


def body(exit_wave, amplitude, probe, offsets, owner):
    areas = lax.axis_size("area")
    columns = lax.axis_size("pos")
    held = exit_wave.shape[0]
    size = exit_wave.shape[-1]
    tail = -(-held // 16) * 16
    payload = pl.pallas_call(
        functools.partial(stage_kernel, held, size),
        out_shape=pltpu.VMEM((2 * held * size + tail, size), BF16),
        in_specs=[SMEM, SMEM, VMEM, VMEM],
        out_specs=VMEM,
        compiler_params=limit(probe, exit_wave),
        name="stage",
    )(
        *[
            pltpu.with_memory_space_constraint(value, pltpu.HBM)
            for value in (offsets.T, owner.T, probe, exit_wave)
        ]
    )
    pieces = gathered(payload, columns)
    mine = jnp.concatenate([offsets, owner], 1).reshape(1, 1, 3 * held)
    meta = lax.all_to_all(
        jnp.broadcast_to(mine, (areas * columns, 1, 3 * held)),
        ("area", "pos"),
        split_axis=0,
        concat_axis=0,
        tiled=True,
    ).reshape(areas * columns, 3 * held)

    powers = pltpu.VMEM((columns + 1, 1, 4 * size, size), F32)
    denom = pl.pallas_call(
        functools.partial(denominators, areas, columns, held, size),
        out_shape=room((held + 1, size, size), F32),
        in_specs=[SMEM, VMEM],
        out_specs=VMEM,
        scratch_shapes=[powers],
        compiler_params=limit(powers),
        name="denominators",
    )(meta, pltpu.with_memory_space_constraint(probe, pltpu.HBM))

    band = room((columns + 1, 2, 2 * size, size), F32)
    whole = not isinstance(band, jax.ShapeDtypeStruct)

    def scratch(count):
        return [
            pltpu.VMEM((count, tail, size), jnp.int32),
            pltpu.SMEM((count, tail, size), jnp.int32),
            pltpu.SemaphoreType.DMA,
        ]

    extra = [] if whole else [band, band]
    canvas = []
    for group in groups_of(pieces):
        waves = [pieces[kind] for kind in group]
        canvas = on_chip(canvas)
        canvas = [
            pl.pallas_call(
                functools.partial(band_kernel, held, size, not canvas, whole),
                out_shape=band,
                in_specs=[VMEM] * (len(waves) + len(canvas)),
                out_specs=VMEM,
                scratch_shapes=scratch(len(waves)),
                input_output_aliases={len(waves): 0} if canvas else {},
                compiler_params=limit(*extra, *([] if whole else waves)),
            )(*on_chip(waves), *canvas)
        ]
    message = room((2 * held + 1, size, size), BF16)
    waves = on_chip([list(pieces.values())[-1]])
    outer, paired, canvas = pl.pallas_call(
        functools.partial(late_kernel, areas, columns, held, size, whole),
        out_shape=(message, message, band),
        in_specs=[SMEM] + [VMEM] * 2,
        out_specs=(VMEM, VMEM, VMEM),
        scratch_shapes=scratch(1) + [pltpu.VMEM((2, 3 * size, size), F32)],
        input_output_aliases={2: 2},
        compiler_params=limit(*extra),
        name="band_late",
    )(meta, *waves, *on_chip(canvas))
    pairs = [(i, i + 1) for i in range(1, areas - 1, 2)]
    outer = lax.ppermute(outer, "area", pairs + [(b, a) for a, b in pairs])
    pairs = [(i, i + 1) for i in range(0, areas - 1, 2)]
    paired = lax.ppermute(paired, "area", pairs + [(b, a) for a, b in pairs])
    own = pl.pallas_call(
        functools.partial(own_kernel, columns, held, size),
        out_shape=room((2 * held + 2, size, size), F32),
        in_specs=[SMEM, VMEM],
        out_specs=VMEM,
        compiler_params=limit(*extra),
        name="own_sums",
    )(meta, *on_chip([canvas]))

    rows = pltpu.VMEM((held * size, 2 * size), BF16)
    proj = pltpu.VMEM((held, 2, size, size), F32)
    return pl.pallas_call(
        functools.partial(final_kernel, areas, columns, held, size),
        out_shape=(
            jax.ShapeDtypeStruct((held, 2, size, size), BF16),
            jax.ShapeDtypeStruct((2, size, size), F32),
        ),
        in_specs=[SMEM] + [VMEM] * 9,
        out_specs=(VMEM, VMEM),
        scratch_shapes=[rows, rows, proj],
        compiler_params=limit(rows, rows, proj, proj, proj, proj, proj),
        name="relax",
    )(
        meta,
        *on_chip([own, outer, paired, denom, exit_wave, amplitude, probe]),
        *on_chip(twiddles(size)),
    )


def groups_of(pieces):
    kinds = list(pieces)[:-1]
    if len(kinds) == 7:
        return [
            [(0, False), (0, True), (1, False), (2, False)],
            [(1, True), (3, False), (2, True)],
        ]
    return [kinds[at : at + 4] for at in range(0, len(kinds), 4)]


def solution(mesh):
    return jax.shard_map(
        body,
        mesh=mesh,
        in_specs=(
            P(("area", "pos"), None, None, None),
            P(("area", "pos"), None, None),
            P(),
            P(("area", "pos"), None),
            P(("area", "pos"), None),
        ),
        out_specs=(P(("area", "pos"), None, None, None), P(None, "area", "pos")),
        check_vma=False,
    )
```

profile of v0, /device:TPU:1, one launch (start us, length us, event | category | flops | bytes accessed | tf_op | source)
XLA Modules:
  0.0 60.5 jit_solution(9234203866598131972)
XLA Ops:
  0.6 1.1 %stage.1.refs_0_ = bf16[1040,128]{1,0:T(8,128)(2,1)S(1)} custom-call(s32[2,4]{1,0:T(2,128)} %bitcast.7, s32[1,4]{1,0:T(1,128)} %bitcast.8, f32[2,128,128]{2,1,0:T(8,128)} %refs_7_.1, bf16[4,2,128,128]{3,2,1,0:T(8,128)(2,1)} %refs_5_.1), custom_call_target="tpu_custom_call" | custom-call | tf_op jit(solution)/shard_map/stage/pallas_call | solution.py:348
  1.8 2.2 %collective-permute-start.2 = (bf16[1040,128]{1,0:T(8,128)(2,1)S(1)}, bf16[1040,128]{1,0:T(8,128)(2,1)}, u32[]{:S(2)}, u32[]{:S(2)}) collective-permute-start(bf16[1040,128]{1,0:T(8,128)(2,1)S(1)} %stage.1.refs_0_), channel_id=1, source_target_pairs={{0,2},{1,3},{2,0},{3,1},{4,6},{5,7},{6,4},{7,5},{8,10},{9,11},{10,... | collective-permute-start | bytes 798728 | tf_op jit(solution)/shard_map/ppermute | solution.py:313
  4.0 2.3 %collective-permute-start.4 = (bf16[1040,128]{1,0:T(8,128)(2,1)S(1)}, bf16[1040,128]{1,0:T(8,128)(2,1)}, u32[]{:S(2)}, u32[]{:S(2)}) collective-permute-start(bf16[1040,128]{1,0:T(8,128)(2,1)S(1)} %stage.1.refs_0_), channel_id=1, source_target_pairs={{0,4},{1,5},{2,6},{3,7},{4,0},{5,1},{6,2},{7,3},{8,12},{9,13},{10,... | collective-permute-start | bytes 798728 | tf_op jit(solution)/shard_map/ppermute | solution.py:313
  6.3 0.0 collective-permute-start
  6.3 1.2 %collective-permute-start.6 = (bf16[1040,128]{1,0:T(8,128)(2,1)S(1)}, bf16[1040,128]{1,0:T(8,128)(2,1)S(1)}, u32[]{:S(2)}, u32[]{:S(2)}) collective-permute-start(bf16[1040,128]{1,0:T(8,128)(2,1)S(1)} %stage.1.refs_0_), channel_id=1, source_target_pairs={{0,1},{1,0},{2,3},{3,2},{4,5},{5,4},{6,7},{7,6},{8,9},{9,8},{10,11... | collective-permute-start | bytes 798728 | tf_op jit(solution)/shard_map/ppermute | solution.py:316
  7.5 7.6 %collective-permute-done.2.refs_2_ = bf16[1040,128]{1,0:T(8,128)(2,1)} collective-permute-done((bf16[1040,128]{1,0:T(8,128)(2,1)S(1)}, bf16[1040,128]{1,0:T(8,128)(2,1)}, u32[]{:S(2)}, u32[]{:S(2)}) %collective-permute-start.2) | collective-permute-done | bytes 266272 | tf_op jit(solution)/shard_map/ppermute | solution.py:313
  15.1 1.1 %collective-permute-start.3 = (bf16[1040,128]{1,0:T(8,128)(2,1)}, bf16[1040,128]{1,0:T(8,128)(2,1)S(1)}, u32[]{:S(2)}, u32[]{:S(2)}) collective-permute-start(bf16[1040,128]{1,0:T(8,128)(2,1)} %collective-permute-done.2.refs_2_), channel_id=1, source_target_pairs={{0,1},{1,0},{2,3},{3,2},{4,5},{5,4},{6,7},{7,6},{8,9},{9,8},{10,11... | collective-permute-start | bytes 798728 | tf_op jit(solution)/shard_map/ppermute | solution.py:316
  16.2 0.0 collective-permute-done.4.refs_3_
  16.2 0.4 collective-permute-start.5
  16.6 6.8 %collective-permute-done.refs_1_ = bf16[1040,128]{1,0:T(8,128)(2,1)S(1)} collective-permute-done((bf16[1040,128]{1,0:T(8,128)(2,1)S(1)}, bf16[1040,128]{1,0:T(8,128)(2,1)S(1)}, u32[]{:S(2)}, u32[]{:S(2)}) %collective-permute-start) | collective-permute-done | bytes 266272 | tf_op jit(solution)/shard_map/ppermute | solution.py:313
  23.4 1.2 %collective-permute-start.1 = (bf16[1040,128]{1,0:T(8,128)(2,1)S(1)}, bf16[1040,128]{1,0:T(8,128)(2,1)S(1)}, u32[]{:S(2)}, u32[]{:S(2)}) collective-permute-start(bf16[1040,128]{1,0:T(8,128)(2,1)S(1)} %collective-permute-done.refs_1_), channel_id=1, source_target_pairs={{0,1},{1,0},{2,3},{3,2},{4,5},{5,4},{6,7},{7,6},{8,9},{9,8},{10,11... | collective-permute-start | bytes 798728 | tf_op jit(solution)/shard_map/ppermute | solution.py:316
  24.6 0.7 %pad_add_fusion = s32[4,3]{0,1:T(4,128)S(1)} fusion(s32[4,1]{0,1:T(1,128)} %param.11, s32[4,2]{0,1:T(2,128)} %param.10), kind=kLoop, calls=%fused_computation | loop fusion | flops 12 | bytes 96 | tf_op jit(solution)/shard_map/concatenate | solution.py:362
  25.3 0.1 copy.12
  25.4 0.1 broadcast_in_dim.7
  25.5 0.6 %broadcast_in_dim.8 = s32[32,1,12]{2,1,0:T(1,128)} broadcast(s32[12]{0:T(128)S(1)} %broadcast_in_dim.7), dimensions={2} | broadcast | bytes 1584 | tf_op jit(solution)/shard_map/broadcast_in_dim | solution.py:364
  26.1 10.3 %all-to-all-start = ((s32[32,1,12]{2,1,0:T(1,128)}), s32[32,1,12]{2,1,0:T(1,128)S(1)}, u32[]{:S(2)}, u32[]{:S(2)}) async-start(s32[32,1,12]{2,1,0:T(1,128)} %broadcast_in_dim.8), calls=%async_computation | async-start | bytes 32768 | tf_op jit(solution)/shard_map/all_to_all | solution.py:363
  36.5 0.0 collective-permute-done.6.refs_1_
  36.5 0.0 copy-start.4
  36.5 0.7 %copy-done.4 = bf16[1040,128]{1,0:T(8,128)(2,1)} copy-done((bf16[1040,128]{1,0:T(8,128)(2,1)}, bf16[1040,128]{1,0:T(8,128)(2,1)S(1)}, u32[]{:S(2)}) %copy-start.4) | copy-done | bytes 266264
  37.2 0.0 copy-start.5
  37.2 0.9 %copy-done.5 = bf16[1040,128]{1,0:T(8,128)(2,1)S(1)} copy-done((bf16[1040,128]{1,0:T(8,128)(2,1)S(1)}, bf16[1040,128]{1,0:T(8,128)(2,1)}, u32[]{:S(2)}) %copy-start.5) | copy-done | bytes 266264
  38.1 3.8 %shard_map.86.refs_3_ = f32[9,2,256,128]{3,2,1,0:T(8,128)S(1)} custom-call(bf16[1040,128]{1,0:T(8,128)(2,1)S(1)} %stage.1.refs_0_, bf16[1040,128]{1,0:T(8,128)(2,1)S(1)} %copy-done.5, bf16[1040,128]{1,0:T(8,128)(2,1)} %collective-permute-done.2.refs_2_, bf16[1040,128]{1,0:T(8,128)(2,1)} %collective-permute-done.4.refs_3_), custom_call_target="tpu_custom_call" | custom-call | tf_op jit(solution)/shard_map/pallas_call | solution.py:398
  41.9 0.0 collective-permute-done.3.refs_0_
  41.9 0.0 collective-permute-done.5.refs_2_
  41.9 3.0 %shard_map.87.refs_2_ = f32[9,2,256,128]{3,2,1,0:T(8,128)S(1)} custom-call(bf16[1040,128]{1,0:T(8,128)(2,1)S(1)} %collective-permute-done.3.refs_0_, bf16[1040,128]{1,0:T(8,128)(2,1)S(1)} %collective-permute-done.refs_1_, bf16[1040,128]{1,0:T(8,128)(2,1)} %collective-permute-done.5.refs_2_, ...), custom_call_target="tpu_custom_call", output_to_operand_aliasing={{}: (3, {})} | custom-call | tf_op jit(solution)/shard_map/pallas_call | solution.py:398
  45.0 0.0 all-to-all-done
  45.0 0.0 collective-permute-done.1.refs_1_
  45.0 2.2 %band_late.1 = (bf16[9,128,128]{2,1,0:T(8,128)(2,1)S(1)}, bf16[9,128,128]{2,1,0:T(8,128)(2,1)S(1)}, f32[9,2,256,128]{3,2,1,0:T(8,128)S(1)}) custom-call(s32[32,12]{1,0:T(8,128)S(1)} %bitcast.3, bf16[1040,128]{1,0:T(8,128)(2,1)S(1)} %collective-permute-done.1.refs_1_, f32[9,2,256,128]{3,2,1,0:T(8,128)S(1)} %shard_map.87.refs_2_), custom_call_target="tpu_custom_call", output_to_operand_aliasing={{2}: (2, {})} | custom-call | tf_op jit(solution)/shard_map/band_late/pallas_call | solution.py:410
  47.3 0.0 copy-start
  47.3 0.0 copy-start.1
  47.3 0.0 copy-start.2
  47.3 0.0 copy-start.3
  47.3 0.0 copy-start.6
  47.3 3.7 %collective-permute-start.7 = (bf16[9,128,128]{2,1,0:T(8,128)(2,1)S(1)}, bf16[9,128,128]{2,1,0:T(8,128)(2,1)S(1)}, u32[]{:S(2)}, u32[]{:S(2)}) collective-permute-start(bf16[9,128,128]{2,1,0:T(8,128)(2,1)S(1)} %get-tuple-element.6), channel_id=1, source_target_pairs={{8,16},{16,8},{9,17},{17,9},{10,18},{18,10},{11,19},{19,11},{12,20... | collective-permute-start | bytes 884744 | tf_op jit(solution)/shard_map/ppermute | solution.py:421
  51.0 0.1 collective-permute-start.8
  51.1 4.5 %denominators.1.refs_4_ = f32[5,128,128]{2,1,0:T(8,128)S(1)} custom-call(s32[32,12]{1,0:T(8,128)S(1)} %bitcast.4, f32[2,128,128]{2,1,0:T(8,128)} %refs_7_.1), custom_call_target="tpu_custom_call" | custom-call | tf_op jit(solution)/shard_map/denominators/pallas_call | solution.py:372
  55.6 1.1 %own_sums.1.refs_1_ = f32[10,128,128]{2,1,0:T(8,128)S(1)} custom-call(s32[32,12]{1,0:T(8,128)S(1)} %bitcast.5, f32[9,2,256,128]{3,2,1,0:T(8,128)S(1)} %get-tuple-element.5.canvas), custom_call_target="tpu_custom_call" | custom-call | tf_op jit(solution)/shard_map/own_sums/pallas_call | solution.py:424
  56.7 0.0 collective-permute-done.7.refs_2_
  56.7 0.0 collective-permute-done.8.refs_3_
  56.7 0.0 copy-done
  56.7 0.0 copy-done.1
  56.7 0.0 copy-done.2
  56.7 0.0 copy-done.3
  56.7 0.0 copy-done.6
  56.7 3.7 %relax.1 = (bf16[4,2,128,128]{3,2,1,0:T(8,128)(2,1)}, f32[2,128,128]{2,1,0:T(8,128)}) custom-call(s32[32,12]{1,0:T(8,128)S(1)} %bitcast.6, f32[10,128,128]{2,1,0:T(8,128)S(1)} %own_sums.1.refs_1_, bf16[9,128,128]{2,1,0:T(8,128)(2,1)S(1)} %collective-permute-done.7.refs_2_, bf16[9,128,128]{2,1,0:T(8,128)(2,1)S(1)} %collective-permute-done.8.refs_3_, ...), custom_call_target="tpu_custom_call" | custom-call | tf_op jit(solution)/shard_map/relax/pallas_call | solution.py:435
Async XLA Ops:
  1.8 13.3 %collective-permute-start.2 = (bf16[1040,128]{1,0:T(8,128)(2,1)S(1)}, bf16[1040,128]{1,0:T(8,128)(2,1)}, u32[]{:S(2)}, u32[]{:S(2)}) collective-permute-start(bf16[1040,128]{1,0:T(8,128)(2,1)S(1)} %stage.1.refs_0_), channel_id=1, source_target_pairs={{0,2},{1,3},{2,0},{3,1},{4,6},{5,7},{6,4},{7,5},{8,10},{9,11},{10,... | collective-permute-start | bytes 798728 | tf_op jit(solution)/shard_map/ppermute | solution.py:313
  4.0 12.3 %collective-permute-start.4 = (bf16[1040,128]{1,0:T(8,128)(2,1)S(1)}, bf16[1040,128]{1,0:T(8,128)(2,1)}, u32[]{:S(2)}, u32[]{:S(2)}) collective-permute-start(bf16[1040,128]{1,0:T(8,128)(2,1)S(1)} %stage.1.refs_0_), channel_id=1, source_target_pairs={{0,4},{1,5},{2,6},{3,7},{4,0},{5,1},{6,2},{7,3},{8,12},{9,13},{10,... | collective-permute-start | bytes 798728 | tf_op jit(solution)/shard_map/ppermute | solution.py:313
  6.3 17.2 %collective-permute-start = (bf16[1040,128]{1,0:T(8,128)(2,1)S(1)}, bf16[1040,128]{1,0:T(8,128)(2,1)S(1)}, u32[]{:S(2)}, u32[]{:S(2)}) collective-permute-start(bf16[1040,128]{1,0:T(8,128)(2,1)S(1)} %stage.1.refs_0_), channel_id=1, source_target_pairs={{0,6},{1,7},{2,4},{3,5},{4,2},{5,3},{6,0},{7,1},{8,14},{9,15},{10,... | collective-permute-start | bytes 798728 | tf_op jit(solution)/shard_map/ppermute | solution.py:313
  6.3 30.2 %collective-permute-start.6 = (bf16[1040,128]{1,0:T(8,128)(2,1)S(1)}, bf16[1040,128]{1,0:T(8,128)(2,1)S(1)}, u32[]{:S(2)}, u32[]{:S(2)}) collective-permute-start(bf16[1040,128]{1,0:T(8,128)(2,1)S(1)} %stage.1.refs_0_), channel_id=1, source_target_pairs={{0,1},{1,0},{2,3},{3,2},{4,5},{5,4},{6,7},{7,6},{8,9},{9,8},{10,11... | collective-permute-start | bytes 798728 | tf_op jit(solution)/shard_map/ppermute | solution.py:316
  15.1 26.8 %collective-permute-start.3 = (bf16[1040,128]{1,0:T(8,128)(2,1)}, bf16[1040,128]{1,0:T(8,128)(2,1)S(1)}, u32[]{:S(2)}, u32[]{:S(2)}) collective-permute-start(bf16[1040,128]{1,0:T(8,128)(2,1)} %collective-permute-done.2.refs_2_), channel_id=1, source_target_pairs={{0,1},{1,0},{2,3},{3,2},{4,5},{5,4},{6,7},{7,6},{8,9},{9,8},{10,11... | collective-permute-start | bytes 798728 | tf_op jit(solution)/shard_map/ppermute | solution.py:316
  16.2 25.7 %collective-permute-start.5 = (bf16[1040,128]{1,0:T(8,128)(2,1)}, bf16[1040,128]{1,0:T(8,128)(2,1)}, u32[]{:S(2)}, u32[]{:S(2)}) collective-permute-start(bf16[1040,128]{1,0:T(8,128)(2,1)} %collective-permute-done.4.refs_3_), channel_id=1, source_target_pairs={{0,1},{1,0},{2,3},{3,2},{4,5},{5,4},{6,7},{7,6},{8,9},{9,8},{10,11... | collective-permute-start | bytes 798728 | tf_op jit(solution)/shard_map/ppermute | solution.py:316
  23.4 21.6 %collective-permute-start.1 = (bf16[1040,128]{1,0:T(8,128)(2,1)S(1)}, bf16[1040,128]{1,0:T(8,128)(2,1)S(1)}, u32[]{:S(2)}, u32[]{:S(2)}) collective-permute-start(bf16[1040,128]{1,0:T(8,128)(2,1)S(1)} %collective-permute-done.refs_1_), channel_id=1, source_target_pairs={{0,1},{1,0},{2,3},{3,2},{4,5},{5,4},{6,7},{7,6},{8,9},{9,8},{10,11... | collective-permute-start | bytes 798728 | tf_op jit(solution)/shard_map/ppermute | solution.py:316
  26.1 18.8 %all-to-all-start = ((s32[32,1,12]{2,1,0:T(1,128)}), s32[32,1,12]{2,1,0:T(1,128)S(1)}, u32[]{:S(2)}, u32[]{:S(2)}) async-start(s32[32,1,12]{2,1,0:T(1,128)} %broadcast_in_dim.8), calls=%async_computation | async-start | bytes 32768 | tf_op jit(solution)/shard_map/all_to_all | solution.py:363
  36.5 0.7 %copy-start.4 = (bf16[1040,128]{1,0:T(8,128)(2,1)}, bf16[1040,128]{1,0:T(8,128)(2,1)S(1)}, u32[]{:S(2)}) copy-start(bf16[1040,128]{1,0:T(8,128)(2,1)S(1)} %collective-permute-done.6.refs_1_) | copy-start | bytes 798724
  37.2 1.0 %copy-start.5 = (bf16[1040,128]{1,0:T(8,128)(2,1)S(1)}, bf16[1040,128]{1,0:T(8,128)(2,1)}, u32[]{:S(2)}) copy-start(bf16[1040,128]{1,0:T(8,128)(2,1)} %copy-done.4) | copy-start | bytes 798724
  47.3 9.4 %copy-start = (f32[2,128,128]{2,1,0:T(8,128)S(1)}, f32[2,128,128]{2,1,0:T(8,128)}, u32[]{:S(2)}) copy-start(f32[2,128,128]{2,1,0:T(8,128)} %refs_7_.1) | copy-start | bytes 393220
  47.3 9.4 %copy-start.1 = (bf16[4,2,128,128]{3,2,1,0:T(8,128)(2,1)S(1)}, bf16[4,2,128,128]{3,2,1,0:T(8,128)(2,1)}, u32[]{:S(2)}) copy-start(bf16[4,2,128,128]{3,2,1,0:T(8,128)(2,1)} %refs_5_.1) | copy-start | bytes 786436
  47.3 9.4 %copy-start.2 = (bf16[2,768,256]{2,1,0:T(8,128)(2,1)S(1)}, bf16[2,768,256]{2,1,0:T(8,128)(2,1)}, u32[]{:S(2)}) copy-start(bf16[2,768,256]{2,1,0:T(8,128)(2,1)} %constant.4.clone.refs_8_) | copy-start | bytes 2359300
  47.3 9.4 %copy-start.3 = (bf16[2,256,768]{2,1,0:T(8,128)(2,1)S(1)}, bf16[2,256,768]{2,1,0:T(8,128)(2,1)}, u32[]{:S(2)}) copy-start(bf16[2,256,768]{2,1,0:T(8,128)(2,1)} %constant.5.clone.refs_9_) | copy-start | bytes 2359300
  47.3 9.4 %copy-start.6 = (bf16[4,128,128]{2,1,0:T(8,128)(2,1)S(1)}, bf16[4,128,128]{2,1,0:T(8,128)(2,1)}, u32[]{:S(2)}) copy-start(bf16[4,128,128]{2,1,0:T(8,128)(2,1)} %refs_6_.1) | copy-start | bytes 393220
  47.3 9.4 %collective-permute-start.7 = (bf16[9,128,128]{2,1,0:T(8,128)(2,1)S(1)}, bf16[9,128,128]{2,1,0:T(8,128)(2,1)S(1)}, u32[]{:S(2)}, u32[]{:S(2)}) collective-permute-start(bf16[9,128,128]{2,1,0:T(8,128)(2,1)S(1)} %get-tuple-element.6), channel_id=1, source_target_pairs={{8,16},{16,8},{9,17},{17,9},{10,18},{18,10},{11,19},{19,11},{12,20... | collective-permute-start | bytes 884744 | tf_op jit(solution)/shard_map/ppermute | solution.py:421
  51.0 5.7 %collective-permute-start.8 = (bf16[9,128,128]{2,1,0:T(8,128)(2,1)S(1)}, bf16[9,128,128]{2,1,0:T(8,128)(2,1)S(1)}, u32[]{:S(2)}, u32[]{:S(2)}) collective-permute-start(bf16[9,128,128]{2,1,0:T(8,128)(2,1)S(1)} %get-tuple-element.7), channel_id=1, source_target_pairs={{0,8},{16,24},{8,0},{24,16},{1,9},{17,25},{9,1},{25,17},{2,10},{18... | collective-permute-start | bytes 884744 | tf_op jit(solution)/shard_map/ppermute | solution.py:423
where the time goes:
time: 60.8 us; the launch traced here: 60.5 us
  starting transfers between devices  22.4 us (37%)
  Pallas kernels  19.5 us (32%)
  waiting for transfers between devices  14.5 us (24%)
  local copies, waits for them, and re-layouts  2.48 us (4%)
  between operations  0.84 us (1%)
  other arithmetic  0.7 us (1%)
    ppermute x3, waiting for transfers between devices, gathered(): pieces[step, False] = lax.ppermute(wave, 'pos', pairs)  14.5 us
    all_to_all x1, starting transfers between devices, body(): lax.all_to_all(jnp.broadcast_to(mine, (areas * columns, 1, 3 * held)), ('...  10.3 us
    pallas_call x2, Pallas kernels, body(): pl.pallas_call(functools.partial(band_kernel, held, size, not canvas, who...  6.81 us
    pallas_call x1, Pallas kernels, body(): pl.pallas_call(functools.partial(denominators, areas, columns, held, size...  4.52 us
    ppermute x3, starting transfers between devices, gathered(): pieces[step, False] = lax.ppermute(wave, 'pos', pairs)  4.49 us
    ppermute x4, starting transfers between devices, gathered(): lax.ppermute(pieces[step, False], 'pos', [(i, i ^ 1) for i in range(colum...  3.89 us
    pallas_call x1, Pallas kernels, body(): pl.pallas_call(functools.partial(final_kernel, areas, columns, held, size...  3.74 us
    ppermute x1, starting transfers between devices, body(): outer = lax.ppermute(outer, 'area', pairs + [(b, a) for a, b in pairs])  3.67 us
  transfers between devices with their start and end apart: 10, of which 2 were waited for; matrix products, arithmetic and copies ran while one was open for 2% of the time, Pallas kernels for 20%

commit v1 on v0

v1 whole, which is shorter than its diff:
```python
import functools
import math

import jax
import jax.numpy as jnp
import numpy as np
from jax import lax
from jax.experimental import pallas as pl
from jax.experimental.pallas import tpu as pltpu
from jax.sharding import PartitionSpec as P


F32 = jnp.float32
BF16 = jnp.bfloat16
VMEM = pl.BlockSpec(memory_space=pltpu.VMEM)
SMEM = pl.BlockSpec(memory_space=pltpu.SMEM)


def lanes_of(rows, size):
    return lax.broadcasted_iota(jnp.int32, (rows, size), 1)


def where_is(meta, device, number):
    return tuple(meta[device, 3 * number + part] for part in range(3))


def place(canvas, tile, channel, row, col, data):
    size = data.shape[0]
    turned = pltpu.roll(data, col, 1)
    wraps = lanes_of(size, size) < col
    rows = pl.ds(row, size)
    canvas[tile, channel, rows, :] += jnp.where(wraps, 0.0, turned)
    canvas[tile + 1, channel, rows, :] += jnp.where(wraps, turned, 0.0)


def cut(canvas, tile, channel, row, col, size):
    rows = pl.ds(row, size)
    here = canvas[tile, channel, rows, :]
    after = canvas[tile + 1, channel, rows, :]
    both = jnp.where(lanes_of(size, size) < col, after, here)
    return pltpu.roll(both, lax.rem(size - col, size), 1)


def tile_part(canvas, tile, channel, row, count, size):
    here = canvas[tile, channel, pl.ds(row, count), :]
    after = canvas[tile + 1, channel, pl.ds(row, count), :]
    half = size // 2
    return pltpu.roll(jnp.where(lanes_of(count, size) < half, after, here), half, 1)


def stage_kernel(held, size, offsets, owner, probe, wave, payload, *halves):
    probe_re = probe[0]
    probe_im = probe[1]
    for number in range(held):
        wave_re = wave[number, 0].astype(F32)
        wave_im = wave[number, 1].astype(F32)
        for channel, part in (
            (0, probe_re * wave_re + probe_im * wave_im),
            (1, probe_re * wave_im - probe_im * wave_re),
        ):
            first = (2 * number + channel) * size
            rounded = part.astype(BF16)
            payload[first : first + size, :] = rounded
            for half in halves:
                if 0 <= first < half.shape[0]:
                    half[first : first + size, :] = rounded
                first -= half.shape[0]
    rows = payload.shape[0] - 2 * held * size
    row_at = lax.broadcasted_iota(jnp.int32, (rows, size), 0)
    col_at = lanes_of(rows, size)
    tail = jnp.zeros((rows, size), jnp.int32)
    for number in range(held):
        for part, value in enumerate((offsets[0, number], offsets[1, number], owner[0, number])):
            tail = jnp.where((row_at == number) & (col_at == part), value, tail)
    payload[2 * held * size :, :] = tail.astype(F32).astype(BF16)


def add_waves(canvas, size, wave, first, count, where):
    def add_one(number, carry):
        row, col, tile = where(first + number)
        for channel in (0, 1):
            at = pl.multiple_of((2 * number + channel) * size, size)
            place(canvas, tile, channel, row, col, wave[pl.ds(at, size), :].astype(F32))
        return carry

    lax.fori_loop(0, count, add_one, 0, unroll=count <= 4)


def place_by_tail(canvas, held, size, waves, numbers, scalars, sem):
    for at, wave in enumerate(waves):
        numbers[at] = wave[2 * held * size :, :].astype(F32).astype(jnp.int32)
    copy = pltpu.make_async_copy(numbers, scalars, sem)
    copy.start()
    copy.wait()
    for at, wave in enumerate(waves):
        add_waves(
            canvas,
            size,
            wave,
            0,
            held,
            lambda number, at=at: tuple(scalars[at, number, part] for part in range(3)),
        )


def place_by_meta(canvas, columns, size, meta, specs, waves):
    inner = 2 if columns % 2 == 0 else 1
    base = lax.axis_index("area") * columns
    for (kind, first, count), wave in zip(specs, waves):
        source = base + source_of(lax.axis_index("pos"), kind, inner, columns)
        add_waves(
            canvas,
            size,
            wave,
            first,
            count,
            lambda number, source=source: where_is(meta, source, number),
        )


def source_of(pos, kind, inner, columns):
    step, swapped = kind
    line = pos // inner
    lines = columns // inner
    if lines & (lines - 1) == 0:
        line = jnp.bitwise_xor(line, step)
    else:
        line = lax.rem(line + lines - step, lines)
    side = lax.rem(pos, inner)
    return line * inner + (inner - 1 - side if swapped else side)


def place_powers(canvas, meta, probe, area, shift, columns, held, size):
    power = probe[0] * probe[0] + probe[1] * probe[1]

    @pl.loop(0, columns)
    def _(source):
        for number in range(held):
            row, col, tile = where_is(meta, area * columns + source, number)
            place(canvas, tile, 0, row + (shift + 1) * size, col, power)


def powers_kernel(columns, held, size, meta, probe, canvas):
    canvas[...] = jnp.zeros_like(canvas)
    place_powers(canvas, meta, probe, lax.axis_index("area"), 0, columns, held, size)


def denominators(areas, columns, held, size, whole, meta, probe, given, share, canvas):
    area = lax.axis_index("area")
    pos = lax.axis_index("pos")
    if not whole:
        canvas[...] = given[...]
    for shift in (-1, 1):
        other = area + shift

        @pl.when((other >= 0) & (other < areas))
        def _(other=other, shift=shift):
            place_powers(canvas, meta, probe, other, shift, columns, held, size)

    half = size // 2
    row_at = lax.broadcasted_iota(jnp.int32, (size, size), 0)
    col_at = lanes_of(size, size)
    for number in range(held):
        row, col, tile = where_is(meta, area * columns + pos, number)
        top = area * size + row - half
        start = tile * size + col - half
        inside = (
            (row_at >= -top)
            & (row_at < areas * size - top)
            & (col_at >= -start)
            & (col_at < columns * size - start)
        )
        sums = cut(canvas, tile, 0, row + size, col, size)
        share[number] = jnp.where(inside, 1.0 / (sums + 0.1), 0.0)
    share[held] = 1.0 / (tile_part(canvas, pos, 0, size + half, size, size) + 0.1)


def first_kernel(held, size, *refs):
    canvas, numbers, scalars, sem = refs[-4:]
    canvas[...] = jnp.zeros_like(canvas)
    place_by_tail(canvas, held, size, refs[:-4], numbers, scalars, sem)


def band_kernel(columns, size, whole, specs, meta, *refs):
    given, canvas = refs[-2:]
    if not whole:
        canvas[...] = given[...]
    place_by_meta(canvas, columns, size, meta, specs, refs[:-2])


def outer_kernel(areas, columns, held, size, whole, specs, meta, *refs):
    given, out, canvas, shifted = refs[-4:]
    if not whole:
        canvas[...] = given[...]
    place_by_meta(canvas, columns, size, meta, specs, refs[:-4])
    cut_message(areas, columns, held, size, meta, canvas, out, shifted, True)


def paired_kernel(areas, columns, held, size, meta, canvas, out, own, shifted):
    cut_message(areas, columns, held, size, meta, canvas, out, shifted, False)
    own_sums(columns, held, size, meta, canvas, own)


def neighbour(area, outer):
    step = 1 - 2 * lax.rem(area, 2)
    return -step if outer else step


def cut_message(areas, columns, held, size, meta, canvas, out, shifted, is_outer):
    area = lax.axis_index("area")
    pos = lax.axis_index("pos")
    half = size // 2
    for side in (0, 1):
        shifted[side, :size] = jnp.zeros((size, size), F32)
        shifted[side, 2 * size :] = jnp.zeros((size, size), F32)
    step = neighbour(area, is_outer)
    above = step < 0
    device = jnp.clip(area + step, 0, areas - 1) * columns + pos
    block = pl.multiple_of(jnp.where(above, 0, size), 8)
    for number in range(held):
        row, col, tile = where_is(meta, device, number)
        for channel in (0, 1):
            shifted[channel, size : 2 * size] = cut(canvas, tile, channel, block, col, size)
            first = jnp.where(above, row, row + size)
            out[2 * number + channel] = shifted[channel, pl.ds(first, size), :].astype(BF16)
    first = pl.multiple_of(jnp.where(above, 0, size + half), 8)
    for channel in (0, 1):
        out[2 * held, channel * half : (channel + 1) * half] = tile_part(
            canvas, pos, channel, first, half, size
        ).astype(BF16)


def own_sums(columns, held, size, meta, canvas, own):
    pos = lax.axis_index("pos")
    me = lax.axis_index("area") * columns + pos
    for number in range(held):
        row, col, tile = where_is(meta, me, number)
        for channel in (0, 1):
            own[2 * number + channel] = cut(canvas, tile, channel, row, col, size)
    for channel in (0, 1):
        own[2 * held + channel] = tile_part(canvas, pos, channel, size // 2, size, size)


def split(value):
    high = value.astype(BF16)
    return (high, (value - high.astype(F32)).astype(BF16))


def dot(left, right):
    return jnp.dot(left, right, preferred_element_type=F32)


def from_right(high, low, matrix):
    size = matrix.shape[1]
    if low is None:
        return dot(jnp.concatenate([high, high], 1), matrix[: 2 * size])
    return dot(jnp.concatenate([high, high, low], 1), matrix)


def from_left(matrix, high, low):
    size = matrix.shape[0]
    if low is None:
        return dot(matrix[:, : 2 * size], jnp.concatenate([high, high], 0))
    return dot(matrix, jnp.concatenate([high, high, low], 0))


def there(rows_high, rows_low, right, left, held, size, chunk):
    results = []
    for first in range(0, held, chunk):
        count = min(chunk, held - first)
        at = slice(first * size, (first + count) * size)
        low = None if rows_low is None else rows_low[at, :]
        mid = to_columns(from_right(rows_high[at, :], low, right), count, size)
        high = mid.astype(BF16)
        low = None if rows_low is None else (mid - high.astype(F32)).astype(BF16)
        results.append(from_left(left, high, low))
    return jnp.concatenate(results, 1)


def to_columns(value, held, size):
    return jnp.concatenate(
        [
            jnp.concatenate(
                [
                    value[number * size : (number + 1) * size, part * size : (part + 1) * size]
                    for number in range(held)
                ],
                1,
            )
            for part in (0, 1)
        ],
        0,
    )


def final_kernel(held, size, *refs):
    own, outer, paired, share, wave, amplitude, probe, right, left = refs[:9]
    new_wave, tile_out, rows_high, rows_low, proj = refs[9:]
    half = size // 2
    odd = lax.rem(lax.axis_index("area"), 2) == 1
    scale = share[held]
    for channel in (0, 1):
        rows = slice(channel * half, (channel + 1) * half)
        sums = own[2 * held + channel]
        one = outer[2 * held, rows].astype(F32)
        two = paired[2 * held, rows].astype(F32)
        sums = sums + jnp.concatenate([jnp.where(odd, two, one), jnp.where(odd, one, two)], 0)
        tile_out[channel] = sums * scale
    probe_re = probe[0]
    probe_im = probe[1]
    for number in range(held):
        patch = []
        for channel in (0, 1):
            at = 2 * number + channel
            sums = own[at] + (outer[at].astype(F32) + paired[at].astype(F32))
            patch.append((sums * share[number]).astype(BF16).astype(F32))
        proj_re = probe_re * patch[0] - probe_im * patch[1]
        proj_im = probe_re * patch[1] + probe_im * patch[0]
        proj[number, 0] = proj_re
        proj[number, 1] = proj_im
        at = slice(number * size, (number + 1) * size)
        for channel, part in ((0, proj_re), (1, proj_im)):
            high, low = split(2.0 * part - wave[number, channel].astype(F32))
            rows_high[at, channel * size : (channel + 1) * size] = high
            rows_low[at, channel * size : (channel + 1) * size] = low
    spectrum = there(rows_high, rows_low, right[0], left[0], held, size, CHUNK)
    for number in range(held):
        at = slice(number * size, (number + 1) * size)
        spec_re = spectrum[:size, at]
        spec_im = spectrum[size:, at]
        ratio = amplitude[number].astype(F32) * lax.rsqrt(
            spec_re * spec_re + spec_im * spec_im + 0.01
        )
        for channel, part in ((0, spec_re), (1, spec_im)):
            high, low = split(part * ratio)
            rows_high[at, channel * size : (channel + 1) * size] = high
            rows_low[at, channel * size : (channel + 1) * size] = low
    back = there(rows_high, rows_low, right[1], left[1], held, size, CHUNK)
    for number in range(held):
        at = slice(number * size, (number + 1) * size)
        for channel in (0, 1):
            new_wave[number, channel] = (
                0.75 * wave[number, channel].astype(F32)
                - 0.5 * proj[number, channel]
                + 0.75 * back[channel * size : (channel + 1) * size, at]
            ).astype(BF16)


def twiddles(size):
    at = np.arange(size)
    angle = 2.0 * math.pi * ((at[:, None] * at[None, :]) % size) / size
    real = np.cos(angle) / math.sqrt(size)
    imag = -np.sin(angle) / math.sqrt(size)

    def parts(whole, axis):
        whole = whole.astype(np.float32)
        high = whole.astype(BF16)
        low = (whole - high.astype(np.float32)).astype(BF16)
        return np.concatenate([high, low, high], axis)

    right = [parts(np.block([[real, im], [-im, real]]), 0) for im in (imag, -imag)]
    left = [parts(np.block([[real, -im], [im, real]]), 1) for im in (imag, -imag)]
    return (jnp.asarray(np.stack(right)), jnp.asarray(np.stack(left)))


def steps_of(lines):
    return sorted(range(1, lines), key=lambda step: (step != lines // 2, step))


def gathered(payload, halves, held, columns):
    inner = 2 if columns % 2 == 0 else 1
    lines = columns // inner
    xor = lines & (lines - 1) == 0
    steps = [0] + steps_of(lines)
    pieces = []

    def send(kind, parts, pairs):
        for first, count, value in parts:
            moved = lax.ppermute(value, "pos", pairs)
            pieces.append((kind, first, count, moved))

    for step in steps:
        pairs = [
            (i, (i // inner ^ step if xor else (i // inner + step) % lines) * inner + i % inner)
            for i in range(columns)
        ]
        parts = halves if step == steps[-1] else [(0, held, payload)]
        if step == 0:
            pieces.append(((0, False), 0, held, payload))
        else:
            send((step, False), parts, pairs)
    if inner == 2:
        pairs = [(i, i ^ 1) for i in range(columns)]
        for kind, *part in list(pieces):
            if xor and lines > 2 and kind[0] == 1:
                along = [(i, (i // inner ^ 1) * inner + i % inner) for i in range(columns)]
                moved = lax.ppermute(beside, "pos", along)
                pieces.append(((1, True), 0, held, moved))
                continue
            moved = lax.ppermute(part[2], "pos", pairs)
            if kind[0] == 0:
                beside = moved
            pieces.append(((kind[0], True), part[0], part[1], moved))
    return pieces


def on_chip(values):
    if sum(value.size * value.dtype.itemsize for value in values) > 2**23:
        return list(values)
    return [pltpu.with_memory_space_constraint(value, pltpu.VMEM) for value in values]


def limit(*values):
    held = sum(math.prod(value.shape) * np.dtype(value.dtype).itemsize for value in values)
    return pltpu.CompilerParams(vmem_limit_bytes=min(held + 2**23, 60 * 2**20))


SMALL = 6 * 2**20
CHUNK = 2


def room(shape, dtype):
    if math.prod(shape) * np.dtype(dtype).itemsize <= SMALL:
        return pltpu.VMEM(shape, dtype)
    return jax.ShapeDtypeStruct(shape, dtype)


def body(exit_wave, amplitude, probe, offsets, owner):
    areas = lax.axis_size("area")
    columns = lax.axis_size("pos")
    held = exit_wave.shape[0]
    size = exit_wave.shape[-1]
    tail = -(-held // 16) * 16
    cuts = [count for count in (held // 2, held - held // 2) if count]
    payload, *halves = pl.pallas_call(
        functools.partial(stage_kernel, held, size),
        out_shape=[room((2 * held * size + tail, size), BF16)]
        + [room((2 * count * size, size), BF16) for count in cuts],
        in_specs=[SMEM, SMEM, VMEM, VMEM],
        out_specs=[VMEM] * (1 + len(cuts)),
        compiler_params=limit(probe, exit_wave),
        name="stage",
    )(
        *[
            pltpu.with_memory_space_constraint(value, pltpu.HBM)
            for value in (offsets.T, owner.T, probe, exit_wave)
        ]
    )
    firsts = [0, cuts[0]]
    pieces = gathered(payload, list(zip(firsts, cuts, halves)), held, columns)
    mine = jnp.concatenate([offsets, owner], 1).reshape(1, 1, 3 * held)
    meta = lax.all_to_all(
        jnp.broadcast_to(mine, (areas * columns, 1, 3 * held)),
        ("area", "pos"),
        split_axis=0,
        concat_axis=0,
        tiled=True,
    ).reshape(areas * columns, 3 * held)

    powers = room((columns + 1, 1, 4 * size, size), F32)
    whole = not isinstance(powers, jax.ShapeDtypeStruct)
    far_probe = pltpu.with_memory_space_constraint(probe, pltpu.HBM)
    weights = pl.pallas_call(
        functools.partial(powers_kernel, columns, held, size),
        out_shape=powers,
        in_specs=[SMEM, VMEM],
        out_specs=VMEM,
        compiler_params=limit(*([] if whole else [powers])),
        name="powers",
    )(meta, far_probe)
    share, _ = pl.pallas_call(
        functools.partial(denominators, areas, columns, held, size, whole),
        out_shape=(room((held + 1, size, size), F32), powers),
        in_specs=[SMEM, VMEM, VMEM],
        out_specs=(VMEM, VMEM),
        input_output_aliases={2: 1},
        compiler_params=limit(*([] if whole else [powers, powers])),
        name="denominators",
    )(meta, far_probe, *on_chip([weights]))

    band = room((columns + 1, 2, 2 * size, size), F32)
    whole = not isinstance(band, jax.ShapeDtypeStruct)

    extra = [] if whole else [band, band]
    first, *groups, late = groups_of(pieces)
    waves = [piece[-1] for piece in first]
    canvas = pl.pallas_call(
        functools.partial(first_kernel, held, size),
        out_shape=band,
        in_specs=[VMEM] * len(waves),
        out_specs=VMEM,
        scratch_shapes=[
            pltpu.VMEM((len(waves), tail, size), jnp.int32),
            pltpu.SMEM((len(waves), tail, size), jnp.int32),
            pltpu.SemaphoreType.DMA,
        ],
        compiler_params=limit(*extra, *([] if whole else waves)),
        name="band0",
    )(*on_chip(waves))
    for group in groups:
        waves = [piece[-1] for piece in group]
        canvas = pl.pallas_call(
            functools.partial(band_kernel, columns, size, whole, [piece[:3] for piece in group]),
            out_shape=band,
            in_specs=[SMEM] + [VMEM] * (len(waves) + 1),
            out_specs=VMEM,
            input_output_aliases={len(waves) + 1: 0},
            compiler_params=limit(*extra, *([] if whole else waves)),
        )(meta, *on_chip(waves), *on_chip([canvas]))
    message = room((2 * held + 1, size, size), BF16)
    waves = [piece[-1] for piece in late]
    shifted = pltpu.VMEM((2, 3 * size, size), F32)
    outer, canvas = pl.pallas_call(
        functools.partial(
            outer_kernel, areas, columns, held, size, whole, [piece[:3] for piece in late]
        ),
        out_shape=(message, band),
        in_specs=[SMEM] + [VMEM] * (len(waves) + 1),
        out_specs=(VMEM, VMEM),
        scratch_shapes=[shifted],
        input_output_aliases={len(waves) + 1: 1},
        compiler_params=limit(*extra),
        name="band_outer",
    )(meta, *on_chip(waves), *on_chip([canvas]))
    pairs = [(i, i + 1) for i in range(1, areas - 1, 2)]
    outer = lax.ppermute(outer, "area", pairs + [(b, a) for a, b in pairs])
    paired, own = pl.pallas_call(
        functools.partial(paired_kernel, areas, columns, held, size),
        out_shape=(message, room((2 * held + 2, size, size), F32)),
        in_specs=[SMEM, VMEM],
        out_specs=(VMEM, VMEM),
        scratch_shapes=[shifted],
        compiler_params=limit(*extra),
        name="band_paired",
    )(meta, *on_chip([canvas]))
    pairs = [(i, i + 1) for i in range(0, areas - 1, 2)]
    paired = lax.ppermute(paired, "area", pairs + [(b, a) for a, b in pairs])

    rows = pltpu.VMEM((held * size, 2 * size), BF16)
    proj = pltpu.VMEM((held, 2, size, size), F32)
    return pl.pallas_call(
        functools.partial(final_kernel, held, size),
        out_shape=(
            jax.ShapeDtypeStruct((held, 2, size, size), BF16),
            jax.ShapeDtypeStruct((2, size, size), F32),
        ),
        in_specs=[VMEM] * 9,
        out_specs=(VMEM, VMEM),
        scratch_shapes=[rows, rows, proj],
        compiler_params=limit(rows, rows, proj, proj, proj, proj, proj),
        name="relax",
    )(
        *on_chip([own, outer, paired, share, exit_wave, amplitude, probe]),
        *on_chip(twiddles(size)),
    )


def groups_of(pieces):
    at = {(kind, first): piece for piece in pieces for kind, first in [piece[:2]]}
    if len(pieces) == 10:
        half = pieces[-1][1]
        order = [
            [((0, False), 0), ((0, True), 0), ((1, False), 0), ((2, False), 0)],
            [((1, True), 0), ((2, True), 0), ((3, False), 0), ((3, False), half)],
            [((3, True), 0), ((3, True), half)],
        ]
        return [[at[key] for key in group] for group in order]
    return [pieces[first : first + 4] for first in range(0, len(pieces), 4)]


def solution(mesh):
    return jax.shard_map(
        body,
        mesh=mesh,
        in_specs=(
            P(("area", "pos"), None, None, None),
            P(("area", "pos"), None, None),
            P(),
            P(("area", "pos"), None),
            P(("area", "pos"), None),
        ),
        out_specs=(P(("area", "pos"), None, None, None), P(None, "area", "pos")),
        check_vma=False,
    )
```

time: 60.8 us -> 63.4 us (1.043)
  waiting for transfers between devices: 14.5 us -> 22.4 us
  Pallas kernels: 19.5 us -> 14.7 us
  starting transfers between devices: 22.4 us -> 20.4 us
  local copies, waits for them, and re-layouts: 2.48 us -> 4.11 us
    ppermute x7 -> x9, waiting for transfers between devices: 14.5 us -> 19.7 us  [the longest x4 19.7 us: send(): moved = lax.ppermute(value, 'pos', pairs)]
    all_to_all x1, starting transfers between devices: 10.3 us -> 5.52 us  [body(): lax.all_to_all(jnp.broadcast_to(mine, (areas * columns, 1, 3 * held)), ('...]
    pallas_call x6 -> x7, Pallas kernels: 15 us -> 11.4 us  [the longest x1 2.36 us: body(): pl.pallas_call(functools.partial(final_kernel, held, size), out_shape=(ja...]
    ppermute x7 -> x9, starting transfers between devices: 8.38 us -> 11.8 us  [the longest x4 7.75 us: send(): moved = lax.ppermute(value, 'pos', pairs)]
    all_to_all x1, waiting for transfers between devices: 0.01 us -> 2.28 us  [body(): lax.all_to_all(jnp.broadcast_to(mine, (areas * columns, 1, 3 * held)), ('...]
    unnamed x14 -> x18, local copies, waits for them, and re-layouts: 1.68 us -> 3.31 us
    ppermute x1, starting transfers between devices: 3.67 us -> 2.29 us  [body(): outer = lax.ppermute(outer, 'area', pairs + [(b, a) for a, b in pairs])]
    pallas_call x1, Pallas kernels: 4.52 us -> 3.31 us  [body(): pl.pallas_call(functools.partial(denominators, areas, columns, held, size...]
  transfers between devices with their start and end apart: 10 -> 12, of which waited for: 2 -> 5; matrix products, arithmetic and copies ran while one was open for 2% -> 2% of each run, Pallas kernels for 20% -> 14%
where the time goes in v1:
time: 63.4 us; the launch traced here: 63.1 us
  waiting for transfers between devices  22.4 us (35%)
  starting transfers between devices  20.4 us (32%)
  Pallas kernels  14.7 us (23%)
  local copies, waits for them, and re-layouts  4.11 us (6%)
  between operations  0.78 us (1%)
  other arithmetic  0.7 us (1%)
    ppermute x4, waiting for transfers between devices, send(): moved = lax.ppermute(value, 'pos', pairs)  19.7 us
    ppermute x4, starting transfers between devices, send(): moved = lax.ppermute(value, 'pos', pairs)  7.75 us
    all_to_all x1, starting transfers between devices, body(): lax.all_to_all(jnp.broadcast_to(mine, (areas * columns, 1, 3 * held)), ('...  5.52 us
    unnamed x18, local copies, waits for them, and re-layouts  3.31 us
    pallas_call x1, Pallas kernels, body(): pl.pallas_call(functools.partial(denominators, areas, columns, held, size...  3.31 us
    ppermute x4, starting transfers between devices, gathered(): moved = lax.ppermute(part[2], 'pos', pairs)  2.7 us
    pallas_call x1, Pallas kernels, body(): pl.pallas_call(functools.partial(final_kernel, held, size), out_shape=(ja...  2.36 us
    ppermute x1, starting transfers between devices, body(): outer = lax.ppermute(outer, 'area', pairs + [(b, a) for a, b in pairs])  2.29 us
  transfers between devices with their start and end apart: 12, of which 5 were waited for; matrix products, arithmetic and copies ran while one was open for 2% of the time, Pallas kernels for 14%

profile of v1, /device:TPU:1, one launch (start us, length us, event | category | flops | bytes accessed | tf_op | source)
XLA Modules:
  0.0 63.1 jit_solution(7133927363365759999)
XLA Ops:
  0.6 1.1 %stage.1 = (bf16[1040,128]{1,0:T(8,128)(2,1)S(1)}, bf16[512,128]{1,0:T(8,128)(2,1)S(1)}, bf16[512,128]{1,0:T(8,128)(2,1)S(1)}) custom-call(s32[2,4]{1,0:T(2,128)} %bitcast.8, s32[1,4]{1,0:T(1,128)} %bitcast.9, f32[2,128,128]{2,1,0:T(8,128)} %refs_6_.1, bf16[4,2,128,128]{3,2,1,0:T(8,128)(2,1)} %refs_4_.1), custom_call_target="tpu_custom_call" | custom-call | tf_op jit(solution)/shard_map/stage/pallas_call | solution.py:435
  1.8 3.2 %collective-permute-start.6 = (bf16[1040,128]{1,0:T(8,128)(2,1)S(1)}, bf16[1040,128]{1,0:T(8,128)(2,1)S(1)}, u32[]{:S(2)}, u32[]{:S(2)}) collective-permute-start(bf16[1040,128]{1,0:T(8,128)(2,1)S(1)} %get-tuple-element.12.refs_0_), channel_id=1, source_target_pairs={{0,4},{1,5},{2,6},{3,7},{4,0},{5,1},{6,2},{7,3},{8,12},{9,13},{10,... | collective-permute-start | bytes 798728 | tf_op jit(solution)/shard_map/ppermute | solution.py:379
  5.0 1.2 %collective-permute-start.4 = (bf16[1040,128]{1,0:T(8,128)(2,1)S(1)}, bf16[1040,128]{1,0:T(8,128)(2,1)S(1)}, u32[]{:S(2)}, u32[]{:S(2)}) collective-permute-start(bf16[1040,128]{1,0:T(8,128)(2,1)S(1)} %get-tuple-element.12.refs_0_), channel_id=1, source_target_pairs={{0,1},{1,0},{2,3},{3,2},{4,5},{5,4},{6,7},{7,6},{8,9},{9,8},{10,11... | collective-permute-start | bytes 798728 | tf_op jit(solution)/shard_map/ppermute | solution.py:400
  6.2 1.3 %collective-permute-start.8 = (bf16[1040,128]{1,0:T(8,128)(2,1)S(1)}, bf16[1040,128]{1,0:T(8,128)(2,1)S(1)}, u32[]{:S(2)}, u32[]{:S(2)}) collective-permute-start(bf16[1040,128]{1,0:T(8,128)(2,1)S(1)} %get-tuple-element.12.refs_0_), channel_id=1, source_target_pairs={{0,2},{1,3},{2,0},{3,1},{4,6},{5,7},{6,4},{7,5},{8,10},{9,11},{10,... | collective-permute-start | bytes 798728 | tf_op jit(solution)/shard_map/ppermute | solution.py:379
  7.5 0.0 copy-start.4
  7.5 0.7 %copy-done.4 = bf16[1040,128]{1,0:T(8,128)(2,1)} copy-done((bf16[1040,128]{1,0:T(8,128)(2,1)}, bf16[1040,128]{1,0:T(8,128)(2,1)S(1)}, u32[]{:S(2)}) %copy-start.4) | copy-done | bytes 266264
  8.2 8.6 %collective-permute-done.6.refs_3_ = bf16[1040,128]{1,0:T(8,128)(2,1)S(1)} collective-permute-done((bf16[1040,128]{1,0:T(8,128)(2,1)S(1)}, bf16[1040,128]{1,0:T(8,128)(2,1)S(1)}, u32[]{:S(2)}, u32[]{:S(2)}) %collective-permute-start.6) | collective-permute-done | bytes 266272 | tf_op jit(solution)/shard_map/ppermute | solution.py:379
  16.8 1.0 %collective-permute-start.7 = (bf16[1040,128]{1,0:T(8,128)(2,1)S(1)}, bf16[1040,128]{1,0:T(8,128)(2,1)S(1)}, u32[]{:S(2)}, u32[]{:S(2)}) collective-permute-start(bf16[1040,128]{1,0:T(8,128)(2,1)S(1)} %collective-permute-done.6.refs_3_), channel_id=1, source_target_pairs={{0,1},{1,0},{2,3},{3,2},{4,5},{5,4},{6,7},{7,6},{8,9},{9,8},{10,11... | collective-permute-start | bytes 798728 | tf_op jit(solution)/shard_map/ppermute | solution.py:400
  17.8 0.0 collective-permute-done.4.refs_1_
  17.8 1.4 %collective-permute-start.5 = (bf16[1040,128]{1,0:T(8,128)(2,1)S(1)}, bf16[1040,128]{1,0:T(8,128)(2,1)S(1)}, u32[]{:S(2)}, u32[]{:S(2)}) collective-permute-start(bf16[1040,128]{1,0:T(8,128)(2,1)S(1)} %collective-permute-done.4.refs_1_), channel_id=1, source_target_pairs={{0,2},{1,3},{2,0},{3,1},{4,6},{5,7},{6,4},{7,5},{8,10},{9,11},{10,... | collective-permute-start | bytes 798728 | tf_op jit(solution)/shard_map/ppermute | solution.py:397
  19.2 2.8 %collective-permute-start = (bf16[512,128]{1,0:T(8,128)(2,1)S(1)}, bf16[512,128]{1,0:T(8,128)(2,1)}, u32[]{:S(2)}, u32[]{:S(2)}) collective-permute-start(bf16[512,128]{1,0:T(8,128)(2,1)S(1)} %get-tuple-element.10), channel_id=1, source_target_pairs={{0,6},{1,7},{2,4},{3,5},{4,2},{5,3},{6,0},{7,1},{8,14},{9,15},{10,... | collective-permute-start | bytes 393224 | tf_op jit(solution)/shard_map/ppermute | solution.py:379
  22.0 0.4 collective-permute-start.2
  22.5 8.5 %collective-permute-done.refs_2_ = bf16[512,128]{1,0:T(8,128)(2,1)} collective-permute-done((bf16[512,128]{1,0:T(8,128)(2,1)S(1)}, bf16[512,128]{1,0:T(8,128)(2,1)}, u32[]{:S(2)}, u32[]{:S(2)}) %collective-permute-start) | collective-permute-done | bytes 131104 | tf_op jit(solution)/shard_map/ppermute | solution.py:379
  30.9 0.2 collective-permute-start.1
  31.2 2.6 %collective-permute-done.2.refs_3_ = bf16[512,128]{1,0:T(8,128)(2,1)} collective-permute-done((bf16[512,128]{1,0:T(8,128)(2,1)S(1)}, bf16[512,128]{1,0:T(8,128)(2,1)}, u32[]{:S(2)}, u32[]{:S(2)}) %collective-permute-start.2) | collective-permute-done | bytes 131104 | tf_op jit(solution)/shard_map/ppermute | solution.py:379
  33.8 0.2 collective-permute-start.3
  34.0 0.7 %pad_add_fusion = s32[4,3]{0,1:T(4,128)S(1)} fusion(s32[4,1]{0,1:T(1,128)} %param.11, s32[4,2]{0,1:T(2,128)} %param.10), kind=kLoop, calls=%fused_computation | loop fusion | flops 12 | bytes 96 | tf_op jit(solution)/shard_map/concatenate | solution.py:451
  34.7 0.1 copy.13
  34.8 0.1 broadcast_in_dim.7
  34.9 0.6 broadcast_in_dim.8
  35.5 5.5 %all-to-all-start = ((s32[32,1,12]{2,1,0:T(1,128)}), s32[32,1,12]{2,1,0:T(1,128)S(1)}, u32[]{:S(2)}, u32[]{:S(2)}) async-start(s32[32,1,12]{2,1,0:T(1,128)} %broadcast_in_dim.8), calls=%async_computation | async-start | bytes 32768 | tf_op jit(solution)/shard_map/all_to_all | solution.py:452
  41.1 0.0 collective-permute-done.8.refs_2_
  41.1 0.0 copy-start.6
  41.1 0.7 %copy-done.6 = bf16[1040,128]{1,0:T(8,128)(2,1)} copy-done((bf16[1040,128]{1,0:T(8,128)(2,1)}, bf16[1040,128]{1,0:T(8,128)(2,1)S(1)}, u32[]{:S(2)}) %copy-start.6) | copy-done | bytes 266264
  41.8 0.9 %copy-done.5 = bf16[1040,128]{1,0:T(8,128)(2,1)S(1)} copy-done((bf16[1040,128]{1,0:T(8,128)(2,1)S(1)}, bf16[1040,128]{1,0:T(8,128)(2,1)}, u32[]{:S(2)}) %copy-start.5) | copy-done | bytes 266264
  42.7 0.9 %copy-done.7 = bf16[1040,128]{1,0:T(8,128)(2,1)S(1)} copy-done((bf16[1040,128]{1,0:T(8,128)(2,1)S(1)}, bf16[1040,128]{1,0:T(8,128)(2,1)}, u32[]{:S(2)}) %copy-start.7) | copy-done | bytes 266264
  43.7 1.7 %band0.1.refs_4_ = f32[9,2,256,128]{3,2,1,0:T(8,128)S(1)} custom-call(bf16[1040,128]{1,0:T(8,128)(2,1)S(1)} %copy-done.5, bf16[1040,128]{1,0:T(8,128)(2,1)S(1)} %collective-permute-done.4.refs_1_, bf16[1040,128]{1,0:T(8,128)(2,1)S(1)} %copy-done.7, bf16[1040,128]{1,0:T(8,128)(2,1)S(1)} %collective-permute-done.6.refs_3_), custom_call_target="tpu_custom_call" | custom-call | tf_op jit(solution)/shard_map/band0/pallas_call | solution.py:487
  45.4 2.3 %all-to-all-done = s32[32,1,12]{2,1,0:T(1,128)S(1)} async-done(((s32[32,1,12]{2,1,0:T(1,128)}), s32[32,1,12]{2,1,0:T(1,128)S(1)}, u32[]{:S(2)}, u32[]{:S(2)}) %all-to-all-start) | async-done | bytes 1568 | tf_op jit(solution)/shard_map/all_to_all | solution.py:452
  47.7 0.0 collective-permute-done.7.refs_1_
  47.7 0.0 collective-permute-done.5.refs_0_
  47.7 1.4 %shard_map.86.refs_2_ = f32[9,2,256,128]{3,2,1,0:T(8,128)S(1)} custom-call(s32[32,12]{1,0:T(8,128)S(1)} %bitcast.3, bf16[1040,128]{1,0:T(8,128)(2,1)S(1)} %collective-permute-done.5.refs_0_, bf16[1040,128]{1,0:T(8,128)(2,1)S(1)} %collective-permute-done.7.refs_1_, bf16[512,128]{1,0:T(8,128)(2,1)} %collective-permute-done.refs_2_, ...), custom_call_target="tpu_custom_call", output_to_operand_aliasing={{}: (5, {})} | custom-call | tf_op jit(solution)/shard_map/pallas_call | solution.py:502
  49.1 0.0 collective-permute-done.1.refs_0_
  49.1 0.0 collective-permute-done.3.refs_1_
  49.1 1.4 %band_outer.1 = (bf16[9,128,128]{2,1,0:T(8,128)(2,1)S(1)}, f32[9,2,256,128]{3,2,1,0:T(8,128)S(1)}) custom-call(s32[32,12]{1,0:T(8,128)S(1)} %bitcast.4, bf16[512,128]{1,0:T(8,128)(2,1)} %collective-permute-done.1.refs_0_, bf16[512,128]{1,0:T(8,128)(2,1)} %collective-permute-done.3.refs_1_, ...), custom_call_target="tpu_custom_call", output_to_operand_aliasing={{1}: (3, {})} | custom-call | tf_op jit(solution)/shard_map/band_outer/pallas_call | solution.py:513
  50.5 1.2 %band_paired.1 = (bf16[9,128,128]{2,1,0:T(8,128)(2,1)S(1)}, f32[10,128,128]{2,1,0:T(8,128)S(1)}) custom-call(s32[32,12]{1,0:T(8,128)S(1)} %bitcast.5, f32[9,2,256,128]{3,2,1,0:T(8,128)S(1)} %get-tuple-element.13.canvas), custom_call_target="tpu_custom_call" | custom-call | tf_op jit(solution)/shard_map/band_paired/pallas_call | solution.py:527
  51.7 0.7 %collective-permute-start.10 = (bf16[9,128,128]{2,1,0:T(8,128)(2,1)S(1)}, bf16[9,128,128]{2,1,0:T(8,128)(2,1)S(1)}, u32[]{:S(2)}, u32[]{:S(2)}) collective-permute-start(bf16[9,128,128]{2,1,0:T(8,128)(2,1)S(1)} %get-tuple-element.16), channel_id=1, source_target_pairs={{0,8},{16,24},{8,0},{24,16},{1,9},{17,25},{9,1},{25,17},{2,10},{18... | collective-permute-start | bytes 884744 | tf_op jit(solution)/shard_map/ppermute | solution.py:537
  52.5 0.0 copy-start.8
  52.5 2.3 %collective-permute-start.9 = (bf16[9,128,128]{2,1,0:T(8,128)(2,1)S(1)}, bf16[9,128,128]{2,1,0:T(8,128)(2,1)S(1)}, u32[]{:S(2)}, u32[]{:S(2)}) collective-permute-start(bf16[9,128,128]{2,1,0:T(8,128)(2,1)S(1)} %get-tuple-element.15), channel_id=1, source_target_pairs={{8,16},{16,8},{9,17},{17,9},{10,18},{18,10},{11,19},{19,11},{12,20... | collective-permute-start | bytes 884744 | tf_op jit(solution)/shard_map/ppermute | solution.py:526
  54.8 2.2 %powers.1.given = f32[9,1,512,128]{3,2,1,0:T(8,128)S(1)} custom-call(s32[32,12]{1,0:T(8,128)S(1)} %bitcast.6, f32[2,128,128]{2,1,0:T(8,128)} %refs_6_.1), custom_call_target="tpu_custom_call" | custom-call | tf_op jit(solution)/shard_map/powers/pallas_call | solution.py:463
  57.0 3.3 %denominators.1 = (f32[5,128,128]{2,1,0:T(8,128)S(1)}, f32[9,1,512,128]{3,2,1,0:T(8,128)S(1)}) custom-call(s32[32,12]{1,0:T(8,128)S(1)} %bitcast.7, f32[2,128,128]{2,1,0:T(8,128)} %refs_6_.1, f32[9,1,512,128]{3,2,1,0:T(8,128)S(1)} %powers.1.given), custom_call_target="tpu_custom_call", output_to_operand_aliasing={{1}: (2, {})} | custom-call | tf_op jit(solution)/shard_map/denominators/pallas_call | solution.py:471
  60.3 0.0 collective-permute-done.10.refs_2_
  60.3 0.4 collective-permute-done.9.refs_1_
  60.7 0.0 copy-done
  60.7 0.0 copy-done.1
  60.7 0.0 copy-done.2
  60.7 0.0 copy-done.3
  60.7 0.0 copy-done.8
  60.7 2.4 %relax.1 = (bf16[4,2,128,128]{3,2,1,0:T(8,128)(2,1)}, f32[2,128,128]{2,1,0:T(8,128)}) custom-call(f32[10,128,128]{2,1,0:T(8,128)S(1)} %get-tuple-element.14.refs_0_, bf16[9,128,128]{2,1,0:T(8,128)(2,1)S(1)} %collective-permute-done.9.refs_1_, bf16[9,128,128]{2,1,0:T(8,128)(2,1)S(1)} %collective-permute-done.10.refs_2_, ...), custom_call_target="tpu_custom_call" | custom-call | tf_op jit(solution)/shard_map/relax/pallas_call | solution.py:541
  (6 shorter events, 0.0 us)
Async XLA Ops:
  1.8 15.0 %collective-permute-start.6 = (bf16[1040,128]{1,0:T(8,128)(2,1)S(1)}, bf16[1040,128]{1,0:T(8,128)(2,1)S(1)}, u32[]{:S(2)}, u32[]{:S(2)}) collective-permute-start(bf16[1040,128]{1,0:T(8,128)(2,1)S(1)} %get-tuple-element.12.refs_0_), channel_id=1, source_target_pairs={{0,4},{1,5},{2,6},{3,7},{4,0},{5,1},{6,2},{7,3},{8,12},{9,13},{10,... | collective-permute-start | bytes 798728 | tf_op jit(solution)/shard_map/ppermute | solution.py:379
  5.0 12.9 %collective-permute-start.4 = (bf16[1040,128]{1,0:T(8,128)(2,1)S(1)}, bf16[1040,128]{1,0:T(8,128)(2,1)S(1)}, u32[]{:S(2)}, u32[]{:S(2)}) collective-permute-start(bf16[1040,128]{1,0:T(8,128)(2,1)S(1)} %get-tuple-element.12.refs_0_), channel_id=1, source_target_pairs={{0,1},{1,0},{2,3},{3,2},{4,5},{5,4},{6,7},{7,6},{8,9},{9,8},{10,11... | collective-permute-start | bytes 798728 | tf_op jit(solution)/shard_map/ppermute | solution.py:400
  6.2 34.9 %collective-permute-start.8 = (bf16[1040,128]{1,0:T(8,128)(2,1)S(1)}, bf16[1040,128]{1,0:T(8,128)(2,1)S(1)}, u32[]{:S(2)}, u32[]{:S(2)}) collective-permute-start(bf16[1040,128]{1,0:T(8,128)(2,1)S(1)} %get-tuple-element.12.refs_0_), channel_id=1, source_target_pairs={{0,2},{1,3},{2,0},{3,1},{4,6},{5,7},{6,4},{7,5},{8,10},{9,11},{10,... | collective-permute-start | bytes 798728 | tf_op jit(solution)/shard_map/ppermute | solution.py:379
  7.5 0.7 %copy-start.4 = (bf16[1040,128]{1,0:T(8,128)(2,1)}, bf16[1040,128]{1,0:T(8,128)(2,1)S(1)}, u32[]{:S(2)}) copy-start(bf16[1040,128]{1,0:T(8,128)(2,1)S(1)} %get-tuple-element.12.refs_0_) | copy-start | bytes 798724
  16.8 30.9 %collective-permute-start.7 = (bf16[1040,128]{1,0:T(8,128)(2,1)S(1)}, bf16[1040,128]{1,0:T(8,128)(2,1)S(1)}, u32[]{:S(2)}, u32[]{:S(2)}) collective-permute-start(bf16[1040,128]{1,0:T(8,128)(2,1)S(1)} %collective-permute-done.6.refs_3_), channel_id=1, source_target_pairs={{0,1},{1,0},{2,3},{3,2},{4,5},{5,4},{6,7},{7,6},{8,9},{9,8},{10,11... | collective-permute-start | bytes 798728 | tf_op jit(solution)/shard_map/ppermute | solution.py:400
  17.8 29.9 %collective-permute-start.5 = (bf16[1040,128]{1,0:T(8,128)(2,1)S(1)}, bf16[1040,128]{1,0:T(8,128)(2,1)S(1)}, u32[]{:S(2)}, u32[]{:S(2)}) collective-permute-start(bf16[1040,128]{1,0:T(8,128)(2,1)S(1)} %collective-permute-done.4.refs_1_), channel_id=1, source_target_pairs={{0,2},{1,3},{2,0},{3,1},{4,6},{5,7},{6,4},{7,5},{8,10},{9,11},{10,... | collective-permute-start | bytes 798728 | tf_op jit(solution)/shard_map/ppermute | solution.py:397
  19.2 11.7 %collective-permute-start = (bf16[512,128]{1,0:T(8,128)(2,1)S(1)}, bf16[512,128]{1,0:T(8,128)(2,1)}, u32[]{:S(2)}, u32[]{:S(2)}) collective-permute-start(bf16[512,128]{1,0:T(8,128)(2,1)S(1)} %get-tuple-element.10), channel_id=1, source_target_pairs={{0,6},{1,7},{2,4},{3,5},{4,2},{5,3},{6,0},{7,1},{8,14},{9,15},{10,... | collective-permute-start | bytes 393224 | tf_op jit(solution)/shard_map/ppermute | solution.py:379
  22.0 11.8 %collective-permute-start.2 = (bf16[512,128]{1,0:T(8,128)(2,1)S(1)}, bf16[512,128]{1,0:T(8,128)(2,1)}, u32[]{:S(2)}, u32[]{:S(2)}) collective-permute-start(bf16[512,128]{1,0:T(8,128)(2,1)S(1)} %get-tuple-element.11), channel_id=1, source_target_pairs={{0,6},{1,7},{2,4},{3,5},{4,2},{5,3},{6,0},{7,1},{8,14},{9,15},{10,... | collective-permute-start | bytes 393224 | tf_op jit(solution)/shard_map/ppermute | solution.py:379
  30.9 18.2 %collective-permute-start.1 = (bf16[512,128]{1,0:T(8,128)(2,1)}, bf16[512,128]{1,0:T(8,128)(2,1)}, u32[]{:S(2)}, u32[]{:S(2)}) collective-permute-start(bf16[512,128]{1,0:T(8,128)(2,1)} %collective-permute-done.refs_2_), channel_id=1, source_target_pairs={{0,1},{1,0},{2,3},{3,2},{4,5},{5,4},{6,7},{7,6},{8,9},{9,8},{10,11... | collective-permute-start | bytes 393224 | tf_op jit(solution)/shard_map/ppermute | solution.py:400
  33.8 15.3 %collective-permute-start.3 = (bf16[512,128]{1,0:T(8,128)(2,1)}, bf16[512,128]{1,0:T(8,128)(2,1)}, u32[]{:S(2)}, u32[]{:S(2)}) collective-permute-start(bf16[512,128]{1,0:T(8,128)(2,1)} %collective-permute-done.2.refs_3_), channel_id=1, source_target_pairs={{0,1},{1,0},{2,3},{3,2},{4,5},{5,4},{6,7},{7,6},{8,9},{9,8},{10,11... | collective-permute-start | bytes 393224 | tf_op jit(solution)/shard_map/ppermute | solution.py:400
  35.5 12.2 %all-to-all-start = ((s32[32,1,12]{2,1,0:T(1,128)}), s32[32,1,12]{2,1,0:T(1,128)S(1)}, u32[]{:S(2)}, u32[]{:S(2)}) async-start(s32[32,1,12]{2,1,0:T(1,128)} %broadcast_in_dim.8), calls=%async_computation | async-start | bytes 32768 | tf_op jit(solution)/shard_map/all_to_all | solution.py:452
  41.1 0.7 %copy-start.6 = (bf16[1040,128]{1,0:T(8,128)(2,1)}, bf16[1040,128]{1,0:T(8,128)(2,1)S(1)}, u32[]{:S(2)}) copy-start(bf16[1040,128]{1,0:T(8,128)(2,1)S(1)} %collective-permute-done.8.refs_2_) | copy-start | bytes 798724
  41.8 1.0 %copy-start.5 = (bf16[1040,128]{1,0:T(8,128)(2,1)S(1)}, bf16[1040,128]{1,0:T(8,128)(2,1)}, u32[]{:S(2)}) copy-start(bf16[1040,128]{1,0:T(8,128)(2,1)} %copy-done.4) | copy-start | bytes 798724
  42.7 1.0 %copy-start.7 = (bf16[1040,128]{1,0:T(8,128)(2,1)S(1)}, bf16[1040,128]{1,0:T(8,128)(2,1)}, u32[]{:S(2)}) copy-start(bf16[1040,128]{1,0:T(8,128)(2,1)} %copy-done.6) | copy-start | bytes 798724
  51.7 8.6 %collective-permute-start.10 = (bf16[9,128,128]{2,1,0:T(8,128)(2,1)S(1)}, bf16[9,128,128]{2,1,0:T(8,128)(2,1)S(1)}, u32[]{:S(2)}, u32[]{:S(2)}) collective-permute-start(bf16[9,128,128]{2,1,0:T(8,128)(2,1)S(1)} %get-tuple-element.16), channel_id=1, source_target_pairs={{0,8},{16,24},{8,0},{24,16},{1,9},{17,25},{9,1},{25,17},{2,10},{18... | collective-permute-start | bytes 884744 | tf_op jit(solution)/shard_map/ppermute | solution.py:537
  52.5 8.2 %copy-start = (f32[2,128,128]{2,1,0:T(8,128)S(1)}, f32[2,128,128]{2,1,0:T(8,128)}, u32[]{:S(2)}) copy-start(f32[2,128,128]{2,1,0:T(8,128)} %refs_6_.1) | copy-start | bytes 393220
  52.5 8.2 %copy-start.1 = (bf16[4,2,128,128]{3,2,1,0:T(8,128)(2,1)S(1)}, bf16[4,2,128,128]{3,2,1,0:T(8,128)(2,1)}, u32[]{:S(2)}) copy-start(bf16[4,2,128,128]{3,2,1,0:T(8,128)(2,1)} %refs_4_.1) | copy-start | bytes 786436
  52.5 8.2 %copy-start.2 = (bf16[2,256,768]{2,1,0:T(8,128)(2,1)S(1)}, bf16[2,256,768]{2,1,0:T(8,128)(2,1)}, u32[]{:S(2)}) copy-start(bf16[2,256,768]{2,1,0:T(8,128)(2,1)} %constant.5.clone.refs_8_) | copy-start | bytes 2359300
  52.5 8.2 %copy-start.3 = (bf16[2,768,256]{2,1,0:T(8,128)(2,1)S(1)}, bf16[2,768,256]{2,1,0:T(8,128)(2,1)}, u32[]{:S(2)}) copy-start(bf16[2,768,256]{2,1,0:T(8,128)(2,1)} %constant.4.clone.refs_7_) | copy-start | bytes 2359300
  52.5 8.2 %copy-start.8 = (bf16[4,128,128]{2,1,0:T(8,128)(2,1)S(1)}, bf16[4,128,128]{2,1,0:T(8,128)(2,1)}, u32[]{:S(2)}) copy-start(bf16[4,128,128]{2,1,0:T(8,128)(2,1)} %refs_5_.1) | copy-start | bytes 393220
  52.5 8.2 %collective-permute-start.9 = (bf16[9,128,128]{2,1,0:T(8,128)(2,1)S(1)}, bf16[9,128,128]{2,1,0:T(8,128)(2,1)S(1)}, u32[]{:S(2)}, u32[]{:S(2)}) collective-permute-start(bf16[9,128,128]{2,1,0:T(8,128)(2,1)S(1)} %get-tuple-element.15), channel_id=1, source_target_pairs={{8,16},{16,8},{9,17},{17,9},{10,18},{18,10},{11,19},{19,11},{12,20... | collective-permute-start | bytes 884744 | tf_op jit(solution)/shard_map/ppermute | solution.py:526

commit v2 on v1

--- a/solution.py
+++ b/solution.py
@@ -48,7 +48,7 @@
     return pltpu.roll(jnp.where(lanes_of(count, size) < half, after, here), half, 1)
 
 
-def stage_kernel(held, size, offsets, owner, probe, wave, payload, *halves):
+def stage_kernel(held, size, offsets, owner, probe, wave, payload):
     probe_re = probe[0]
     probe_im = probe[1]
     for number in range(held):
@@ -59,12 +59,7 @@
             (1, probe_re * wave_im - probe_im * wave_re),
         ):
             first = (2 * number + channel) * size
-            rounded = part.astype(BF16)
-            payload[first : first + size, :] = rounded
-            for half in halves:
-                if 0 <= first < half.shape[0]:
-                    half[first : first + size, :] = rounded
-                first -= half.shape[0]
+            payload[first : first + size, :] = part.astype(BF16)
     rows = payload.shape[0] - 2 * held * size
     row_at = lax.broadcasted_iota(jnp.int32, (rows, size), 0)
     col_at = lanes_of(rows, size)
@@ -73,6 +68,13 @@
         for part, value in enumerate((offsets[0, number], offsets[1, number], owner[0, number])):
             tail = jnp.where((row_at == number) & (col_at == part), value, tail)
     payload[2 * held * size :, :] = tail.astype(F32).astype(BF16)
+
+
+def halve_kernel(payload, *halves):
+    first = 0
+    for half in halves:
+        half[...] = payload[first : first + half.shape[0], :]
+        first += half.shape[0]
 
 
 def add_waves(canvas, size, wave, first, count, where):
@@ -432,12 +434,11 @@
     size = exit_wave.shape[-1]
     tail = -(-held // 16) * 16
     cuts = [count for count in (held // 2, held - held // 2) if count]
-    payload, *halves = pl.pallas_call(
+    payload = pl.pallas_call(
         functools.partial(stage_kernel, held, size),
-        out_shape=[room((2 * held * size + tail, size), BF16)]
-        + [room((2 * count * size, size), BF16) for count in cuts],
+        out_shape=room((2 * held * size + tail, size), BF16),
         in_specs=[SMEM, SMEM, VMEM, VMEM],
-        out_specs=[VMEM] * (1 + len(cuts)),
+        out_specs=VMEM,
         compiler_params=limit(probe, exit_wave),
         name="stage",
     )(
@@ -446,6 +447,14 @@
             for value in (offsets.T, owner.T, probe, exit_wave)
         ]
     )
+    halves = pl.pallas_call(
+        halve_kernel,
+        out_shape=[room((2 * count * size, size), BF16) for count in cuts],
+        in_specs=[VMEM],
+        out_specs=[VMEM] * len(cuts),
+        compiler_params=limit(payload, payload),
+        name="halve",
+    )(payload)
     firsts = [0, cuts[0]]
     pieces = gathered(payload, list(zip(firsts, cuts, halves)), held, columns)
     mine = jnp.concatenate([offsets, owner], 1).reshape(1, 1, 3 * held)

time: 63.4 us -> 63.5 us (level)
  local copies, waits for them, and re-layouts: 4.11 us -> 2.48 us
  Pallas kernels: 14.7 us -> 15.7 us
  waiting for transfers between devices: 22.4 us -> 23.2 us
    unnamed x18 -> x14, local copies, waits for them, and re-layouts: 3.31 us -> 1.68 us
    pallas_call x1, Pallas kernels: 1.75 us -> 2.69 us  [body(): pl.pallas_call(functools.partial(first_kernel, held, size), out_shape=ban...]
    ppermute x4, waiting for transfers between devices: 19.7 us -> 20.5 us  [send(): moved = lax.ppermute(value, 'pos', pairs)]
  transfers between devices with their start and end apart: 12 -> 12, of which waited for: 5 -> 5; matrix products, arithmetic and copies ran while one was open for 2% -> 2% of each run, Pallas kernels for 14% -> 15%
where the time goes in v2:
time: 63.5 us; the launch traced here: 63.1 us
  waiting for transfers between devices  23.2 us (37%)
  starting transfers between devices  20.3 us (32%)
  Pallas kernels  15.7 us (25%)
  local copies, waits for them, and re-layouts  2.48 us (4%)
  between operations  0.78 us (1%)
  other arithmetic  0.7 us (1%)
    ppermute x4, waiting for transfers between devices, send(): moved = lax.ppermute(value, 'pos', pairs)  20.5 us
    ppermute x4, starting transfers between devices, send(): moved = lax.ppermute(value, 'pos', pairs)  7.82 us
    all_to_all x1, starting transfers between devices, body(): lax.all_to_all(jnp.broadcast_to(mine, (areas * columns, 1, 3 * held)), ('...  5.42 us
    pallas_call x1, Pallas kernels, body(): pl.pallas_call(functools.partial(denominators, areas, columns, held, size...  3.31 us
    ppermute x4, starting transfers between devices, gathered(): moved = lax.ppermute(part[2], 'pos', pairs)  2.7 us
    pallas_call x1, Pallas kernels, body(): pl.pallas_call(functools.partial(first_kernel, held, size), out_shape=ban...  2.69 us
    pallas_call x1, Pallas kernels, body(): pl.pallas_call(functools.partial(final_kernel, held, size), out_shape=(ja...  2.36 us
    ppermute x1, starting transfers between devices, body(): outer = lax.ppermute(outer, 'area', pairs + [(b, a) for a, b in pairs])  2.29 us
  transfers between devices with their start and end apart: 12, of which 5 were waited for; matrix products, arithmetic and copies ran while one was open for 2% of the time, Pallas kernels for 15%

profile of v2, /device:TPU:1, one launch (start us, length us, event | category | flops | bytes accessed | tf_op | source)
XLA Modules:
  0.0 63.1 jit_solution(2527901825464520641)
XLA Ops:
  0.6 1.1 %stage.1.payload.refs_0_ = bf16[1040,128]{1,0:T(8,128)(2,1)S(1)} custom-call(s32[2,4]{1,0:T(2,128)} %bitcast.8, s32[1,4]{1,0:T(1,128)} %bitcast.9, f32[2,128,128]{2,1,0:T(8,128)} %refs_6_.1, bf16[4,2,128,128]{3,2,1,0:T(8,128)(2,1)} %refs_4_.1), custom_call_target="tpu_custom_call" | custom-call | tf_op jit(solution)/shard_map/stage/pallas_call | solution.py:437
  1.8 3.2 %collective-permute-start.6 = (bf16[1040,128]{1,0:T(8,128)(2,1)S(1)}, bf16[1040,128]{1,0:T(8,128)(2,1)S(1)}, u32[]{:S(2)}, u32[]{:S(2)}) collective-permute-start(bf16[1040,128]{1,0:T(8,128)(2,1)S(1)} %stage.1.payload.refs_0_), channel_id=1, source_target_pairs={{0,4},{1,5},{2,6},{3,7},{4,0},{5,1},{6,2},{7,3},{8,12},{9,13},{10,... | collective-permute-start | bytes 798728 | tf_op jit(solution)/shard_map/ppermute | solution.py:381
  5.0 1.2 %collective-permute-start.4 = (bf16[1040,128]{1,0:T(8,128)(2,1)S(1)}, bf16[1040,128]{1,0:T(8,128)(2,1)}, u32[]{:S(2)}, u32[]{:S(2)}) collective-permute-start(bf16[1040,128]{1,0:T(8,128)(2,1)S(1)} %stage.1.payload.refs_0_), channel_id=1, source_target_pairs={{0,1},{1,0},{2,3},{3,2},{4,5},{5,4},{6,7},{7,6},{8,9},{9,8},{10,11... | collective-permute-start | bytes 798728 | tf_op jit(solution)/shard_map/ppermute | solution.py:402
  6.2 1.3 %collective-permute-start.8 = (bf16[1040,128]{1,0:T(8,128)(2,1)S(1)}, bf16[1040,128]{1,0:T(8,128)(2,1)S(1)}, u32[]{:S(2)}, u32[]{:S(2)}) collective-permute-start(bf16[1040,128]{1,0:T(8,128)(2,1)S(1)} %stage.1.payload.refs_0_), channel_id=1, source_target_pairs={{0,2},{1,3},{2,0},{3,1},{4,6},{5,7},{6,4},{7,5},{8,10},{9,11},{10,... | collective-permute-start | bytes 798728 | tf_op jit(solution)/shard_map/ppermute | solution.py:381
  7.5 9.3 %collective-permute-done.6.refs_3_ = bf16[1040,128]{1,0:T(8,128)(2,1)S(1)} collective-permute-done((bf16[1040,128]{1,0:T(8,128)(2,1)S(1)}, bf16[1040,128]{1,0:T(8,128)(2,1)S(1)}, u32[]{:S(2)}, u32[]{:S(2)}) %collective-permute-start.6) | collective-permute-done | bytes 266272 | tf_op jit(solution)/shard_map/ppermute | solution.py:381
  16.8 1.0 %collective-permute-start.7 = (bf16[1040,128]{1,0:T(8,128)(2,1)S(1)}, bf16[1040,128]{1,0:T(8,128)(2,1)S(1)}, u32[]{:S(2)}, u32[]{:S(2)}) collective-permute-start(bf16[1040,128]{1,0:T(8,128)(2,1)S(1)} %collective-permute-done.6.refs_3_), channel_id=1, source_target_pairs={{0,1},{1,0},{2,3},{3,2},{4,5},{5,4},{6,7},{7,6},{8,9},{9,8},{10,11... | collective-permute-start | bytes 798728 | tf_op jit(solution)/shard_map/ppermute | solution.py:402
  17.8 0.0 collective-permute-done.4.refs_1_
  17.8 1.4 %collective-permute-start.5 = (bf16[1040,128]{1,0:T(8,128)(2,1)}, bf16[1040,128]{1,0:T(8,128)(2,1)S(1)}, u32[]{:S(2)}, u32[]{:S(2)}) collective-permute-start(bf16[1040,128]{1,0:T(8,128)(2,1)} %collective-permute-done.4.refs_1_), channel_id=1, source_target_pairs={{0,2},{1,3},{2,0},{3,1},{4,6},{5,7},{6,4},{7,5},{8,10},{9,11},{10,... | collective-permute-start | bytes 798728 | tf_op jit(solution)/shard_map/ppermute | solution.py:399
  19.2 2.9 %collective-permute-start = (bf16[512,128]{1,0:T(8,128)(2,1)S(1)}, bf16[512,128]{1,0:T(8,128)(2,1)}, u32[]{:S(2)}, u32[]{:S(2)}) collective-permute-start(bf16[512,128]{1,0:T(8,128)(2,1)S(1)} %get-tuple-element.9), channel_id=1, source_target_pairs={{0,6},{1,7},{2,4},{3,5},{4,2},{5,3},{6,0},{7,1},{8,14},{9,15},{10,... | collective-permute-start | bytes 393224 | tf_op jit(solution)/shard_map/ppermute | solution.py:381
  22.1 0.4 collective-permute-start.2
  22.5 8.6 %collective-permute-done.refs_2_ = bf16[512,128]{1,0:T(8,128)(2,1)} collective-permute-done((bf16[512,128]{1,0:T(8,128)(2,1)S(1)}, bf16[512,128]{1,0:T(8,128)(2,1)}, u32[]{:S(2)}, u32[]{:S(2)}) %collective-permute-start) | collective-permute-done | bytes 131104 | tf_op jit(solution)/shard_map/ppermute | solution.py:381
  31.1 0.2 collective-permute-start.1
  31.4 2.6 %collective-permute-done.2.refs_3_ = bf16[512,128]{1,0:T(8,128)(2,1)} collective-permute-done((bf16[512,128]{1,0:T(8,128)(2,1)S(1)}, bf16[512,128]{1,0:T(8,128)(2,1)}, u32[]{:S(2)}, u32[]{:S(2)}) %collective-permute-start.2) | collective-permute-done | bytes 131104 | tf_op jit(solution)/shard_map/ppermute | solution.py:381
  34.0 0.2 collective-permute-start.3
  34.2 0.7 %pad_add_fusion = s32[4,3]{0,1:T(4,128)S(1)} fusion(s32[4,1]{0,1:T(1,128)} %param.11, s32[4,2]{0,1:T(2,128)} %param.10), kind=kLoop, calls=%fused_computation | loop fusion | flops 12 | bytes 96 | tf_op jit(solution)/shard_map/concatenate | solution.py:460
  34.9 0.1 copy.13
  35.0 0.1 broadcast_in_dim.7
  35.1 0.6 broadcast_in_dim.8
  35.7 5.4 %all-to-all-start = ((s32[32,1,12]{2,1,0:T(1,128)}), s32[32,1,12]{2,1,0:T(1,128)S(1)}, u32[]{:S(2)}, u32[]{:S(2)}) async-start(s32[32,1,12]{2,1,0:T(1,128)} %broadcast_in_dim.8), calls=%async_computation | async-start | bytes 32768 | tf_op jit(solution)/shard_map/all_to_all | solution.py:461
  41.1 0.0 collective-permute-done.8.refs_2_
  41.1 0.0 copy-start.4
  41.2 0.7 %copy-done.4 = bf16[1040,128]{1,0:T(8,128)(2,1)} copy-done((bf16[1040,128]{1,0:T(8,128)(2,1)}, bf16[1040,128]{1,0:T(8,128)(2,1)S(1)}, u32[]{:S(2)}) %copy-start.4) | copy-done | bytes 266264
  41.9 0.0 copy-start.5
  41.9 0.9 %copy-done.5 = bf16[1040,128]{1,0:T(8,128)(2,1)S(1)} copy-done((bf16[1040,128]{1,0:T(8,128)(2,1)S(1)}, bf16[1040,128]{1,0:T(8,128)(2,1)}, u32[]{:S(2)}) %copy-start.5) | copy-done | bytes 266264
  42.8 2.7 %band0.1.refs_4_ = f32[9,2,256,128]{3,2,1,0:T(8,128)S(1)} custom-call(bf16[1040,128]{1,0:T(8,128)(2,1)S(1)} %stage.1.payload.refs_0_, bf16[1040,128]{1,0:T(8,128)(2,1)} %collective-permute-done.4.refs_1_, bf16[1040,128]{1,0:T(8,128)(2,1)S(1)} %copy-done.5, bf16[1040,128]{1,0:T(8,128)(2,1)S(1)} %collective-permute-done.6.refs_3_), custom_call_target="tpu_custom_call" | custom-call | tf_op jit(solution)/shard_map/band0/pallas_call | solution.py:496
  45.5 2.3 %all-to-all-done = s32[32,1,12]{2,1,0:T(1,128)S(1)} async-done(((s32[32,1,12]{2,1,0:T(1,128)}), s32[32,1,12]{2,1,0:T(1,128)S(1)}, u32[]{:S(2)}, u32[]{:S(2)}) %all-to-all-start) | async-done | bytes 1568 | tf_op jit(solution)/shard_map/all_to_all | solution.py:461
  47.8 0.0 collective-permute-done.7.refs_1_
  47.8 0.0 collective-permute-done.5.refs_0_
  47.8 1.4 %shard_map.86.refs_2_ = f32[9,2,256,128]{3,2,1,0:T(8,128)S(1)} custom-call(s32[32,12]{1,0:T(8,128)S(1)} %bitcast.3, bf16[1040,128]{1,0:T(8,128)(2,1)S(1)} %collective-permute-done.5.refs_0_, bf16[1040,128]{1,0:T(8,128)(2,1)S(1)} %collective-permute-done.7.refs_1_, bf16[512,128]{1,0:T(8,128)(2,1)} %collective-permute-done.refs_2_, ...), custom_call_target="tpu_custom_call", output_to_operand_aliasing={{}: (5, {})} | custom-call | tf_op jit(solution)/shard_map/pallas_call | solution.py:511
  49.2 0.0 collective-permute-done.1.refs_0_
  49.2 0.0 collective-permute-done.3.refs_1_
  49.2 1.4 %band_outer.1 = (bf16[9,128,128]{2,1,0:T(8,128)(2,1)S(1)}, f32[9,2,256,128]{3,2,1,0:T(8,128)S(1)}) custom-call(s32[32,12]{1,0:T(8,128)S(1)} %bitcast.4, bf16[512,128]{1,0:T(8,128)(2,1)} %collective-permute-done.1.refs_0_, bf16[512,128]{1,0:T(8,128)(2,1)} %collective-permute-done.3.refs_1_, ...), custom_call_target="tpu_custom_call", output_to_operand_aliasing={{1}: (3, {})} | custom-call | tf_op jit(solution)/shard_map/band_outer/pallas_call | solution.py:522
  50.6 1.2 %band_paired.1 = (bf16[9,128,128]{2,1,0:T(8,128)(2,1)S(1)}, f32[10,128,128]{2,1,0:T(8,128)S(1)}) custom-call(s32[32,12]{1,0:T(8,128)S(1)} %bitcast.5, f32[9,2,256,128]{3,2,1,0:T(8,128)S(1)} %get-tuple-element.11.canvas), custom_call_target="tpu_custom_call" | custom-call | tf_op jit(solution)/shard_map/band_paired/pallas_call | solution.py:536
  51.8 0.7 %collective-permute-start.10 = (bf16[9,128,128]{2,1,0:T(8,128)(2,1)S(1)}, bf16[9,128,128]{2,1,0:T(8,128)(2,1)S(1)}, u32[]{:S(2)}, u32[]{:S(2)}) collective-permute-start(bf16[9,128,128]{2,1,0:T(8,128)(2,1)S(1)} %get-tuple-element.14), channel_id=1, source_target_pairs={{0,8},{16,24},{8,0},{24,16},{1,9},{17,25},{9,1},{25,17},{2,10},{18... | collective-permute-start | bytes 884744 | tf_op jit(solution)/shard_map/ppermute | solution.py:546
  52.6 0.0 copy-start
  52.6 0.0 copy-start.1
  52.6 0.0 copy-start.6
  52.6 2.3 %collective-permute-start.9 = (bf16[9,128,128]{2,1,0:T(8,128)(2,1)S(1)}, bf16[9,128,128]{2,1,0:T(8,128)(2,1)S(1)}, u32[]{:S(2)}, u32[]{:S(2)}) collective-permute-start(bf16[9,128,128]{2,1,0:T(8,128)(2,1)S(1)} %get-tuple-element.13), channel_id=1, source_target_pairs={{8,16},{16,8},{9,17},{17,9},{10,18},{18,10},{11,19},{19,11},{12,20... | collective-permute-start | bytes 884744 | tf_op jit(solution)/shard_map/ppermute | solution.py:535
  54.9 2.2 %powers.1.given = f32[9,1,512,128]{3,2,1,0:T(8,128)S(1)} custom-call(s32[32,12]{1,0:T(8,128)S(1)} %bitcast.6, f32[2,128,128]{2,1,0:T(8,128)} %refs_6_.1), custom_call_target="tpu_custom_call" | custom-call | tf_op jit(solution)/shard_map/powers/pallas_call | solution.py:472
  57.1 3.3 %denominators.1 = (f32[5,128,128]{2,1,0:T(8,128)S(1)}, f32[9,1,512,128]{3,2,1,0:T(8,128)S(1)}) custom-call(s32[32,12]{1,0:T(8,128)S(1)} %bitcast.7, f32[2,128,128]{2,1,0:T(8,128)} %refs_6_.1, f32[9,1,512,128]{3,2,1,0:T(8,128)S(1)} %powers.1.given), custom_call_target="tpu_custom_call", output_to_operand_aliasing={{1}: (2, {})} | custom-call | tf_op jit(solution)/shard_map/denominators/pallas_call | solution.py:480
  60.4 0.0 collective-permute-done.10.refs_2_
  60.4 0.4 collective-permute-done.9.refs_1_
  60.8 0.0 copy-done
  60.8 0.0 copy-done.1
  60.8 0.0 copy-done.2
  60.8 0.0 copy-done.3
  60.8 0.0 copy-done.6
  60.8 2.4 %relax.1 = (bf16[4,2,128,128]{3,2,1,0:T(8,128)(2,1)}, f32[2,128,128]{2,1,0:T(8,128)}) custom-call(f32[10,128,128]{2,1,0:T(8,128)S(1)} %get-tuple-element.12.refs_0_, bf16[9,128,128]{2,1,0:T(8,128)(2,1)S(1)} %collective-permute-done.9.refs_1_, bf16[9,128,128]{2,1,0:T(8,128)(2,1)S(1)} %collective-permute-done.10.refs_2_, ...), custom_call_target="tpu_custom_call" | custom-call | tf_op jit(solution)/shard_map/relax/pallas_call | solution.py:550
  (3 shorter events, 0.0 us)
Async XLA Ops:
  1.8 15.0 %collective-permute-start.6 = (bf16[1040,128]{1,0:T(8,128)(2,1)S(1)}, bf16[1040,128]{1,0:T(8,128)(2,1)S(1)}, u32[]{:S(2)}, u32[]{:S(2)}) collective-permute-start(bf16[1040,128]{1,0:T(8,128)(2,1)S(1)} %stage.1.payload.refs_0_), channel_id=1, source_target_pairs={{0,4},{1,5},{2,6},{3,7},{4,0},{5,1},{6,2},{7,3},{8,12},{9,13},{10,... | collective-permute-start | bytes 798728 | tf_op jit(solution)/shard_map/ppermute | solution.py:381
  5.0 12.9 %collective-permute-start.4 = (bf16[1040,128]{1,0:T(8,128)(2,1)S(1)}, bf16[1040,128]{1,0:T(8,128)(2,1)}, u32[]{:S(2)}, u32[]{:S(2)}) collective-permute-start(bf16[1040,128]{1,0:T(8,128)(2,1)S(1)} %stage.1.payload.refs_0_), channel_id=1, source_target_pairs={{0,1},{1,0},{2,3},{3,2},{4,5},{5,4},{6,7},{7,6},{8,9},{9,8},{10,11... | collective-permute-start | bytes 798728 | tf_op jit(solution)/shard_map/ppermute | solution.py:402
  6.2 35.0 %collective-permute-start.8 = (bf16[1040,128]{1,0:T(8,128)(2,1)S(1)}, bf16[1040,128]{1,0:T(8,128)(2,1)S(1)}, u32[]{:S(2)}, u32[]{:S(2)}) collective-permute-start(bf16[1040,128]{1,0:T(8,128)(2,1)S(1)} %stage.1.payload.refs_0_), channel_id=1, source_target_pairs={{0,2},{1,3},{2,0},{3,1},{4,6},{5,7},{6,4},{7,5},{8,10},{9,11},{10,... | collective-permute-start | bytes 798728 | tf_op jit(solution)/shard_map/ppermute | solution.py:381
  16.8 31.0 %collective-permute-start.7 = (bf16[1040,128]{1,0:T(8,128)(2,1)S(1)}, bf16[1040,128]{1,0:T(8,128)(2,1)S(1)}, u32[]{:S(2)}, u32[]{:S(2)}) collective-permute-start(bf16[1040,128]{1,0:T(8,128)(2,1)S(1)} %collective-permute-done.6.refs_3_), channel_id=1, source_target_pairs={{0,1},{1,0},{2,3},{3,2},{4,5},{5,4},{6,7},{7,6},{8,9},{9,8},{10,11... | collective-permute-start | bytes 798728 | tf_op jit(solution)/shard_map/ppermute | solution.py:402
  17.8 30.0 %collective-permute-start.5 = (bf16[1040,128]{1,0:T(8,128)(2,1)}, bf16[1040,128]{1,0:T(8,128)(2,1)S(1)}, u32[]{:S(2)}, u32[]{:S(2)}) collective-permute-start(bf16[1040,128]{1,0:T(8,128)(2,1)} %collective-permute-done.4.refs_1_), channel_id=1, source_target_pairs={{0,2},{1,3},{2,0},{3,1},{4,6},{5,7},{6,4},{7,5},{8,10},{9,11},{10,... | collective-permute-start | bytes 798728 | tf_op jit(solution)/shard_map/ppermute | solution.py:399
  19.2 11.9 %collective-permute-start = (bf16[512,128]{1,0:T(8,128)(2,1)S(1)}, bf16[512,128]{1,0:T(8,128)(2,1)}, u32[]{:S(2)}, u32[]{:S(2)}) collective-permute-start(bf16[512,128]{1,0:T(8,128)(2,1)S(1)} %get-tuple-element.9), channel_id=1, source_target_pairs={{0,6},{1,7},{2,4},{3,5},{4,2},{5,3},{6,0},{7,1},{8,14},{9,15},{10,... | collective-permute-start | bytes 393224 | tf_op jit(solution)/shard_map/ppermute | solution.py:381
  22.1 11.9 %collective-permute-start.2 = (bf16[512,128]{1,0:T(8,128)(2,1)S(1)}, bf16[512,128]{1,0:T(8,128)(2,1)}, u32[]{:S(2)}, u32[]{:S(2)}) collective-permute-start(bf16[512,128]{1,0:T(8,128)(2,1)S(1)} %get-tuple-element.10), channel_id=1, source_target_pairs={{0,6},{1,7},{2,4},{3,5},{4,2},{5,3},{6,0},{7,1},{8,14},{9,15},{10,... | collective-permute-start | bytes 393224 | tf_op jit(solution)/shard_map/ppermute | solution.py:381
  31.1 18.1 %collective-permute-start.1 = (bf16[512,128]{1,0:T(8,128)(2,1)}, bf16[512,128]{1,0:T(8,128)(2,1)}, u32[]{:S(2)}, u32[]{:S(2)}) collective-permute-start(bf16[512,128]{1,0:T(8,128)(2,1)} %collective-permute-done.refs_2_), channel_id=1, source_target_pairs={{0,1},{1,0},{2,3},{3,2},{4,5},{5,4},{6,7},{7,6},{8,9},{9,8},{10,11... | collective-permute-start | bytes 393224 | tf_op jit(solution)/shard_map/ppermute | solution.py:402
  34.0 15.2 %collective-permute-start.3 = (bf16[512,128]{1,0:T(8,128)(2,1)}, bf16[512,128]{1,0:T(8,128)(2,1)}, u32[]{:S(2)}, u32[]{:S(2)}) collective-permute-start(bf16[512,128]{1,0:T(8,128)(2,1)} %collective-permute-done.2.refs_3_), channel_id=1, source_target_pairs={{0,1},{1,0},{2,3},{3,2},{4,5},{5,4},{6,7},{7,6},{8,9},{9,8},{10,11... | collective-permute-start | bytes 393224 | tf_op jit(solution)/shard_map/ppermute | solution.py:402
  35.7 12.1 %all-to-all-start = ((s32[32,1,12]{2,1,0:T(1,128)}), s32[32,1,12]{2,1,0:T(1,128)S(1)}, u32[]{:S(2)}, u32[]{:S(2)}) async-start(s32[32,1,12]{2,1,0:T(1,128)} %broadcast_in_dim.8), calls=%async_computation | async-start | bytes 32768 | tf_op jit(solution)/shard_map/all_to_all | solution.py:461
  41.1 0.7 %copy-start.4 = (bf16[1040,128]{1,0:T(8,128)(2,1)}, bf16[1040,128]{1,0:T(8,128)(2,1)S(1)}, u32[]{:S(2)}) copy-start(bf16[1040,128]{1,0:T(8,128)(2,1)S(1)} %collective-permute-done.8.refs_2_) | copy-start | bytes 798724
  41.9 1.0 %copy-start.5 = (bf16[1040,128]{1,0:T(8,128)(2,1)S(1)}, bf16[1040,128]{1,0:T(8,128)(2,1)}, u32[]{:S(2)}) copy-start(bf16[1040,128]{1,0:T(8,128)(2,1)} %copy-done.4) | copy-start | bytes 798724
  51.8 8.6 %collective-permute-start.10 = (bf16[9,128,128]{2,1,0:T(8,128)(2,1)S(1)}, bf16[9,128,128]{2,1,0:T(8,128)(2,1)S(1)}, u32[]{:S(2)}, u32[]{:S(2)}) collective-permute-start(bf16[9,128,128]{2,1,0:T(8,128)(2,1)S(1)} %get-tuple-element.14), channel_id=1, source_target_pairs={{0,8},{16,24},{8,0},{24,16},{1,9},{17,25},{9,1},{25,17},{2,10},{18... | collective-permute-start | bytes 884744 | tf_op jit(solution)/shard_map/ppermute | solution.py:546
  52.6 8.2 %copy-start = (f32[2,128,128]{2,1,0:T(8,128)S(1)}, f32[2,128,128]{2,1,0:T(8,128)}, u32[]{:S(2)}) copy-start(f32[2,128,128]{2,1,0:T(8,128)} %refs_6_.1) | copy-start | bytes 393220
  52.6 8.2 %copy-start.1 = (bf16[4,2,128,128]{3,2,1,0:T(8,128)(2,1)S(1)}, bf16[4,2,128,128]{3,2,1,0:T(8,128)(2,1)}, u32[]{:S(2)}) copy-start(bf16[4,2,128,128]{3,2,1,0:T(8,128)(2,1)} %refs_4_.1) | copy-start | bytes 786436
  52.6 8.2 %copy-start.2 = (bf16[2,256,768]{2,1,0:T(8,128)(2,1)S(1)}, bf16[2,256,768]{2,1,0:T(8,128)(2,1)}, u32[]{:S(2)}) copy-start(bf16[2,256,768]{2,1,0:T(8,128)(2,1)} %constant.5.clone.refs_8_) | copy-start | bytes 2359300
  52.6 8.2 %copy-start.3 = (bf16[2,768,256]{2,1,0:T(8,128)(2,1)S(1)}, bf16[2,768,256]{2,1,0:T(8,128)(2,1)}, u32[]{:S(2)}) copy-start(bf16[2,768,256]{2,1,0:T(8,128)(2,1)} %constant.4.clone.refs_7_) | copy-start | bytes 2359300
  52.6 8.2 %copy-start.6 = (bf16[4,128,128]{2,1,0:T(8,128)(2,1)S(1)}, bf16[4,128,128]{2,1,0:T(8,128)(2,1)}, u32[]{:S(2)}) copy-start(bf16[4,128,128]{2,1,0:T(8,128)(2,1)} %refs_5_.1) | copy-start | bytes 393220
  52.6 8.2 %collective-permute-start.9 = (bf16[9,128,128]{2,1,0:T(8,128)(2,1)S(1)}, bf16[9,128,128]{2,1,0:T(8,128)(2,1)S(1)}, u32[]{:S(2)}, u32[]{:S(2)}) collective-permute-start(bf16[9,128,128]{2,1,0:T(8,128)(2,1)S(1)} %get-tuple-element.13), channel_id=1, source_target_pairs={{8,16},{16,8},{9,17},{17,9},{10,18},{18,10},{11,19},{19,11},{12,20... | collective-permute-start | bytes 884744 | tf_op jit(solution)/shard_map/ppermute | solution.py:535

commit v3 on v2

--- a/solution.py
+++ b/solution.py
@@ -49,17 +49,10 @@
 
 
 def stage_kernel(held, size, offsets, owner, probe, wave, payload):
-    probe_re = probe[0]
-    probe_im = probe[1]
-    for number in range(held):
-        wave_re = wave[number, 0].astype(F32)
-        wave_im = wave[number, 1].astype(F32)
-        for channel, part in (
-            (0, probe_re * wave_re + probe_im * wave_im),
-            (1, probe_re * wave_im - probe_im * wave_re),
-        ):
+    for number in range(held):
+        for channel, part in enumerate(weighted(probe, wave[number, 0], wave[number, 1])):
             first = (2 * number + channel) * size
-            payload[first : first + size, :] = part.astype(BF16)
+            payload[first : first + size, :] = part
     rows = payload.shape[0] - 2 * held * size
     row_at = lax.broadcasted_iota(jnp.int32, (rows, size), 0)
     col_at = lanes_of(rows, size)
@@ -77,15 +70,28 @@
         first += half.shape[0]
 
 
-def add_waves(canvas, size, wave, first, count, where):
+def add_waves(canvas, size, wave, first, count, where, probe=None):
     def add_one(number, carry):
         row, col, tile = where(first + number)
-        for channel in (0, 1):
-            at = pl.multiple_of((2 * number + channel) * size, size)
-            place(canvas, tile, channel, row, col, wave[pl.ds(at, size), :].astype(F32))
+        if probe is None:
+            for channel in (0, 1):
+                at = pl.multiple_of((2 * number + channel) * size, size)
+                place(canvas, tile, channel, row, col, wave[pl.ds(at, size), :].astype(F32))
+        else:
+            parts = weighted(probe, wave[number, 0], wave[number, 1])
+            for channel, part in enumerate(parts):
+                place(canvas, tile, channel, row, col, part.astype(F32))
         return carry
 
     lax.fori_loop(0, count, add_one, 0, unroll=count <= 4)
+
+
+def weighted(probe, wave_re, wave_im):
+    wave_re = wave_re.astype(F32)
+    wave_im = wave_im.astype(F32)
+    first = probe[0] * wave_re + probe[1] * wave_im
+    second = probe[0] * wave_im - probe[1] * wave_re
+    return (first.astype(BF16), second.astype(BF16))
 
 
 def place_by_tail(canvas, held, size, waves, numbers, scalars, sem):
@@ -105,7 +111,7 @@
         )
 
 
-def place_by_meta(canvas, columns, size, meta, specs, waves):
+def place_by_meta(canvas, columns, size, meta, probe, specs, waves):
     inner = 2 if columns % 2 == 0 else 1
     base = lax.axis_index("area") * columns
     for (kind, first, count), wave in zip(specs, waves):
@@ -117,6 +123,7 @@
             first,
             count,
             lambda number, source=source: where_is(meta, source, number),
+            probe if len(wave.shape) == 4 else None,
         )
 
 
@@ -183,18 +190,18 @@
     place_by_tail(canvas, held, size, refs[:-4], numbers, scalars, sem)
 
 
-def band_kernel(columns, size, whole, specs, meta, *refs):
+def band_kernel(columns, size, whole, specs, meta, probe, *refs):
     given, canvas = refs[-2:]
     if not whole:
         canvas[...] = given[...]
-    place_by_meta(canvas, columns, size, meta, specs, refs[:-2])
+    place_by_meta(canvas, columns, size, meta, probe, specs, refs[:-2])
 
 
 def outer_kernel(areas, columns, held, size, whole, specs, meta, *refs):
     given, out, canvas, shifted = refs[-4:]
     if not whole:
         canvas[...] = given[...]
-    place_by_meta(canvas, columns, size, meta, specs, refs[:-4])
+    place_by_meta(canvas, columns, size, meta, None, specs, refs[:-4])
     cut_message(areas, columns, held, size, meta, canvas, out, shifted, True)
 
 
@@ -369,7 +376,7 @@
     return sorted(range(1, lines), key=lambda step: (step != lines // 2, step))
 
 
-def gathered(payload, halves, held, columns):
+def gathered(raw, payload, halves, held, columns):
     inner = 2 if columns % 2 == 0 else 1
     lines = columns // inner
     xor = lines & (lines - 1) == 0
@@ -386,7 +393,7 @@
             (i, (i // inner ^ step if xor else (i // inner + step) % lines) * inner + i % inner)
             for i in range(columns)
         ]
-        parts = halves if step == steps[-1] else [(0, held, payload)]
+        parts = halves if step == steps[-1] else [(0, held, raw if step == steps[1] else payload)]
         if step == 0:
             pieces.append(((0, False), 0, held, payload))
         else:
@@ -456,7 +463,7 @@
         name="halve",
     )(payload)
     firsts = [0, cuts[0]]
-    pieces = gathered(payload, list(zip(firsts, cuts, halves)), held, columns)
+    pieces = gathered(exit_wave, payload, list(zip(firsts, cuts, halves)), held, columns)
     mine = jnp.concatenate([offsets, owner], 1).reshape(1, 1, 3 * held)
     meta = lax.all_to_all(
         jnp.broadcast_to(mine, (areas * columns, 1, 3 * held)),
@@ -511,11 +518,11 @@
         canvas = pl.pallas_call(
             functools.partial(band_kernel, columns, size, whole, [piece[:3] for piece in group]),
             out_shape=band,
-            in_specs=[SMEM] + [VMEM] * (len(waves) + 1),
+            in_specs=[SMEM] + [VMEM] * (len(waves) + 2),
             out_specs=VMEM,
-            input_output_aliases={len(waves) + 1: 0},
-            compiler_params=limit(*extra, *([] if whole else waves)),
-        )(meta, *on_chip(waves), *on_chip([canvas]))
+            input_output_aliases={len(waves) + 2: 0},
+            compiler_params=limit(*extra, probe, *([] if whole else waves)),
+        )(meta, far_probe, *on_chip(waves), *on_chip([canvas]))
     message = room((2 * held + 1, size, size), BF16)
     waves = [piece[-1] for piece in late]
     shifted = pltpu.VMEM((2, 3 * size, size), F32)
@@ -569,12 +576,12 @@
     if len(pieces) == 10:
         half = pieces[-1][1]
         order = [
-            [((0, False), 0), ((0, True), 0), ((1, False), 0), ((2, False), 0)],
-            [((1, True), 0), ((2, True), 0), ((3, False), 0), ((3, False), half)],
+            [((0, False), 0), ((0, True), 0), ((1, False), 0)],
+            [((2, False), 0), ((1, True), 0), ((2, True), 0), ((3, False), 0), ((3, False), half)],
             [((3, True), 0), ((3, True), half)],
         ]
         return [[at[key] for key in group] for group in order]
-    return [pieces[first : first + 4] for first in range(0, len(pieces), 4)]
+    return [pieces[:1]] + [pieces[first : first + 4] for first in range(1, len(pieces), 4)]
 
 
 def solution(mesh):

time: 63.5 us -> 61.3 us (0.965)
  local copies, waits for them, and re-layouts: 2.48 us -> 0.82 us
  starting transfers between devices: 20.3 us -> 21.9 us
  waiting for transfers between devices: 23.2 us -> 21.9 us
  Pallas kernels: 15.7 us -> 14.9 us
    ppermute x4, waiting for transfers between devices: 20.5 us -> 13.8 us  [send(): moved = lax.ppermute(value, 'pos', pairs)]
    all_to_all x1, waiting for transfers between devices: 2.28 us -> 5.16 us  [body(): lax.all_to_all(jnp.broadcast_to(mine, (areas * columns, 1, 3 * held)), ('...]
    ppermute x4, waiting for transfers between devices: 0.01 us -> 2.5 us  [gathered(): moved = lax.ppermute(part[2], 'pos', pairs)]
    unnamed x14 -> x10, local copies, waits for them, and re-layouts: 1.68 us -> 0.02 us
    pallas_call x1, Pallas kernels: 2.69 us -> 1.48 us  [body(): pl.pallas_call(functools.partial(first_kernel, held, size), out_shape=ban...]
    ppermute x4, starting transfers between devices: 2.7 us -> 3.56 us  [gathered(): moved = lax.ppermute(part[2], 'pos', pairs)]
  transfers between devices with their start and end apart: 12 -> 12, of which waited for: 5 -> 6; matrix products, arithmetic and copies ran while one was open for 2% -> 2% of each run, Pallas kernels for 15% -> 14%
where the time goes in v3:
time: 61.3 us; the launch traced here: 61 us
  starting transfers between devices  21.9 us (36%)
  waiting for transfers between devices  21.9 us (36%)
  Pallas kernels  14.9 us (24%)
  local copies, waits for them, and re-layouts  0.82 us (1%)
  between operations  0.77 us (1%)
  other arithmetic  0.7 us (1%)
    ppermute x4, waiting for transfers between devices, send(): moved = lax.ppermute(value, 'pos', pairs)  13.8 us
    ppermute x4, starting transfers between devices, send(): moved = lax.ppermute(value, 'pos', pairs)  7.91 us
    all_to_all x1, starting transfers between devices, body(): lax.all_to_all(jnp.broadcast_to(mine, (areas * columns, 1, 3 * held)), ('...  6.04 us
    all_to_all x1, waiting for transfers between devices, body(): lax.all_to_all(jnp.broadcast_to(mine, (areas * columns, 1, 3 * held)), ('...  5.16 us
    ppermute x4, starting transfers between devices, gathered(): moved = lax.ppermute(part[2], 'pos', pairs)  3.56 us
    pallas_call x1, Pallas kernels, body(): pl.pallas_call(functools.partial(denominators, areas, columns, held, size...  3.31 us
    ppermute x4, waiting for transfers between devices, gathered(): moved = lax.ppermute(part[2], 'pos', pairs)  2.5 us
    pallas_call x1, Pallas kernels, body(): pl.pallas_call(functools.partial(final_kernel, held, size), out_shape=(ja...  2.36 us
  transfers between devices with their start and end apart: 12, of which 6 were waited for; matrix products, arithmetic and copies ran while one was open for 2% of the time, Pallas kernels for 14%

profile of v3, /device:TPU:1, one launch (start us, length us, event | category | flops | bytes accessed | tf_op | source)
XLA Modules:
  0.0 61.0 jit_solution(4594685181056362272)
XLA Ops:
  0.6 1.1 %stage.1.payload.refs_0_ = bf16[1040,128]{1,0:T(8,128)(2,1)S(1)} custom-call(s32[2,4]{1,0:T(2,128)} %bitcast.8, s32[1,4]{1,0:T(1,128)} %bitcast.9, f32[2,128,128]{2,1,0:T(8,128)} %refs_6_.1, bf16[4,2,128,128]{3,2,1,0:T(8,128)(2,1)} %refs_4_.1), custom_call_target="tpu_custom_call" | custom-call | tf_op jit(solution)/shard_map/stage/pallas_call | solution.py:444
  1.8 2.1 %collective-permute-start.5 = (bf16[1040,128]{1,0:T(8,128)(2,1)S(1)}, bf16[1040,128]{1,0:T(8,128)(2,1)S(1)}, u32[]{:S(2)}, u32[]{:S(2)}) collective-permute-start(bf16[1040,128]{1,0:T(8,128)(2,1)S(1)} %stage.1.payload.refs_0_), channel_id=1, source_target_pairs={{0,1},{1,0},{2,3},{3,2},{4,5},{5,4},{6,7},{7,6},{8,9},{9,8},{10,11... | collective-permute-start | bytes 798728 | tf_op jit(solution)/shard_map/ppermute | solution.py:409
  3.9 2.3 %collective-permute-start.4 = (bf16[4,2,128,128]{3,2,1,0:T(8,128)(2,1)}, bf16[4,2,128,128]{3,2,1,0:T(8,128)(2,1)}, u32[]{:S(2)}, u32[]{:S(2)}) collective-permute-start(bf16[4,2,128,128]{3,2,1,0:T(8,128)(2,1)} %refs_4_.1), channel_id=1, source_target_pairs={{0,4},{1,5},{2,6},{3,7},{4,0},{5,1},{6,2},{7,3},{8,12},{9,13},{10,... | collective-permute-start | bytes 786440 | tf_op jit(solution)/shard_map/ppermute | solution.py:388
  6.2 1.3 %collective-permute-start.8 = (bf16[1040,128]{1,0:T(8,128)(2,1)S(1)}, bf16[1040,128]{1,0:T(8,128)(2,1)S(1)}, u32[]{:S(2)}, u32[]{:S(2)}) collective-permute-start(bf16[1040,128]{1,0:T(8,128)(2,1)S(1)} %stage.1.payload.refs_0_), channel_id=1, source_target_pairs={{0,2},{1,3},{2,0},{3,1},{4,6},{5,7},{6,4},{7,5},{8,10},{9,11},{10,... | collective-permute-start | bytes 798728 | tf_op jit(solution)/shard_map/ppermute | solution.py:388
  7.5 2.5 %collective-permute-done.5.refs_1_ = bf16[1040,128]{1,0:T(8,128)(2,1)S(1)} collective-permute-done((bf16[1040,128]{1,0:T(8,128)(2,1)S(1)}, bf16[1040,128]{1,0:T(8,128)(2,1)S(1)}, u32[]{:S(2)}, u32[]{:S(2)}) %collective-permute-start.5) | collective-permute-done | bytes 266272 | tf_op jit(solution)/shard_map/ppermute | solution.py:409
  10.0 1.4 %collective-permute-start.6 = (bf16[1040,128]{1,0:T(8,128)(2,1)S(1)}, bf16[1040,128]{1,0:T(8,128)(2,1)S(1)}, u32[]{:S(2)}, u32[]{:S(2)}) collective-permute-start(bf16[1040,128]{1,0:T(8,128)(2,1)S(1)} %collective-permute-done.5.refs_1_), channel_id=1, source_target_pairs={{0,2},{1,3},{2,0},{3,1},{4,6},{5,7},{6,4},{7,5},{8,10},{9,11},{10,... | collective-permute-start | bytes 798728 | tf_op jit(solution)/shard_map/ppermute | solution.py:406
  11.4 6.6 %collective-permute-done.4.refs_0_ = bf16[4,2,128,128]{3,2,1,0:T(8,128)(2,1)} collective-permute-done((bf16[4,2,128,128]{3,2,1,0:T(8,128)(2,1)}, bf16[4,2,128,128]{3,2,1,0:T(8,128)(2,1)}, u32[]{:S(2)}, u32[]{:S(2)}) %collective-permute-start.4) | collective-permute-done | bytes 262176 | tf_op jit(solution)/shard_map/ppermute | solution.py:388
  18.0 0.2 collective-permute-start.7
  18.2 4.3 %collective-permute-start = (bf16[512,128]{1,0:T(8,128)(2,1)S(1)}, bf16[512,128]{1,0:T(8,128)(2,1)}, u32[]{:S(2)}, u32[]{:S(2)}) collective-permute-start(bf16[512,128]{1,0:T(8,128)(2,1)S(1)} %get-tuple-element.9), channel_id=1, source_target_pairs={{0,6},{1,7},{2,4},{3,5},{4,2},{5,3},{6,0},{7,1},{8,14},{9,15},{10,... | collective-permute-start | bytes 393224 | tf_op jit(solution)/shard_map/ppermute | solution.py:388
  22.4 0.0 collective-permute-start.2
  22.5 4.9 %collective-permute-done.refs_3_ = bf16[512,128]{1,0:T(8,128)(2,1)} collective-permute-done((bf16[512,128]{1,0:T(8,128)(2,1)S(1)}, bf16[512,128]{1,0:T(8,128)(2,1)}, u32[]{:S(2)}, u32[]{:S(2)}) %collective-permute-start) | collective-permute-done | bytes 131104 | tf_op jit(solution)/shard_map/ppermute | solution.py:388
  27.3 0.5 collective-permute-start.1
  27.8 2.4 %collective-permute-done.2.refs_4_ = bf16[512,128]{1,0:T(8,128)(2,1)} collective-permute-done((bf16[512,128]{1,0:T(8,128)(2,1)S(1)}, bf16[512,128]{1,0:T(8,128)(2,1)}, u32[]{:S(2)}, u32[]{:S(2)}) %collective-permute-start.2) | collective-permute-done | bytes 131104 | tf_op jit(solution)/shard_map/ppermute | solution.py:388
  30.2 0.8 %collective-permute-start.3 = (bf16[512,128]{1,0:T(8,128)(2,1)}, bf16[512,128]{1,0:T(8,128)(2,1)}, u32[]{:S(2)}, u32[]{:S(2)}) collective-permute-start(bf16[512,128]{1,0:T(8,128)(2,1)} %collective-permute-done.2.refs_4_), channel_id=1, source_target_pairs={{0,1},{1,0},{2,3},{3,2},{4,5},{5,4},{6,7},{7,6},{8,9},{9,8},{10,11... | collective-permute-start | bytes 393224 | tf_op jit(solution)/shard_map/ppermute | solution.py:409
  31.0 0.7 %pad_add_fusion = s32[4,3]{0,1:T(4,128)S(1)} fusion(s32[4,1]{0,1:T(1,128)} %param.11, s32[4,2]{0,1:T(2,128)} %param.10), kind=kLoop, calls=%fused_computation | loop fusion | flops 12 | bytes 96 | tf_op jit(solution)/shard_map/concatenate | solution.py:467
  31.7 0.1 copy.13
  31.8 0.1 broadcast_in_dim.7
  31.8 0.6 %broadcast_in_dim.8 = s32[32,1,12]{2,1,0:T(1,128)} broadcast(s32[12]{0:T(128)S(1)} %broadcast_in_dim.7), dimensions={2} | broadcast | bytes 1584 | tf_op jit(solution)/shard_map/broadcast_in_dim | solution.py:469
  32.5 6.0 %all-to-all-start = ((s32[32,1,12]{2,1,0:T(1,128)}), s32[32,1,12]{2,1,0:T(1,128)S(1)}, u32[]{:S(2)}, u32[]{:S(2)}) async-start(s32[32,1,12]{2,1,0:T(1,128)} %broadcast_in_dim.8), calls=%async_computation | async-start | bytes 32768 | tf_op jit(solution)/shard_map/all_to_all | solution.py:468
  38.5 0.0 collective-permute-done.8.refs_2_
  38.5 1.5 %band0.1.refs_5_ = f32[9,2,256,128]{3,2,1,0:T(8,128)S(1)} custom-call(bf16[1040,128]{1,0:T(8,128)(2,1)S(1)} %stage.1.payload.refs_0_, bf16[1040,128]{1,0:T(8,128)(2,1)S(1)} %collective-permute-done.5.refs_1_, bf16[1040,128]{1,0:T(8,128)(2,1)S(1)} %collective-permute-done.8.refs_2_), custom_call_target="tpu_custom_call" | custom-call | tf_op jit(solution)/shard_map/band0/pallas_call | solution.py:503
  40.0 5.2 %all-to-all-done = s32[32,1,12]{2,1,0:T(1,128)S(1)} async-done(((s32[32,1,12]{2,1,0:T(1,128)}), s32[32,1,12]{2,1,0:T(1,128)S(1)}, u32[]{:S(2)}, u32[]{:S(2)}) %all-to-all-start) | async-done | bytes 1568 | tf_op jit(solution)/shard_map/all_to_all | solution.py:468
  45.2 0.0 collective-permute-done.7.refs_2_
  45.2 0.0 collective-permute-done.6.refs_1_
  45.2 1.8 %shard_map.86.refs_2_ = f32[9,2,256,128]{3,2,1,0:T(8,128)S(1)} custom-call(s32[32,12]{1,0:T(8,128)S(1)} %bitcast.3, f32[2,128,128]{2,1,0:T(8,128)} %refs_6_.1, bf16[4,2,128,128]{3,2,1,0:T(8,128)(2,1)} %collective-permute-done.4.refs_0_, bf16[1040,128]{1,0:T(8,128)(2,1)S(1)} %collective-permute-done.6.refs_1_, ...), custom_call_target="tpu_custom_call", output_to_operand_aliasing={{}: (7, {})} | custom-call | tf_op jit(solution)/shard_map/pallas_call | solution.py:518
  47.0 0.0 collective-permute-done.1.refs_0_
  47.0 0.0 collective-permute-done.3.refs_1_
  47.0 1.4 %band_outer.1 = (bf16[9,128,128]{2,1,0:T(8,128)(2,1)S(1)}, f32[9,2,256,128]{3,2,1,0:T(8,128)S(1)}) custom-call(s32[32,12]{1,0:T(8,128)S(1)} %bitcast.4, bf16[512,128]{1,0:T(8,128)(2,1)} %collective-permute-done.1.refs_0_, bf16[512,128]{1,0:T(8,128)(2,1)} %collective-permute-done.3.refs_1_, ...), custom_call_target="tpu_custom_call", output_to_operand_aliasing={{1}: (3, {})} | custom-call | tf_op jit(solution)/shard_map/band_outer/pallas_call | solution.py:529
  48.4 1.2 %band_paired.1 = (bf16[9,128,128]{2,1,0:T(8,128)(2,1)S(1)}, f32[10,128,128]{2,1,0:T(8,128)S(1)}) custom-call(s32[32,12]{1,0:T(8,128)S(1)} %bitcast.5, f32[9,2,256,128]{3,2,1,0:T(8,128)S(1)} %get-tuple-element.11.canvas), custom_call_target="tpu_custom_call" | custom-call | tf_op jit(solution)/shard_map/band_paired/pallas_call | solution.py:543
  49.6 0.8 %collective-permute-start.10 = (bf16[9,128,128]{2,1,0:T(8,128)(2,1)S(1)}, bf16[9,128,128]{2,1,0:T(8,128)(2,1)S(1)}, u32[]{:S(2)}, u32[]{:S(2)}) collective-permute-start(bf16[9,128,128]{2,1,0:T(8,128)(2,1)S(1)} %get-tuple-element.14), channel_id=1, source_target_pairs={{0,8},{16,24},{8,0},{24,16},{1,9},{17,25},{9,1},{25,17},{2,10},{18... | collective-permute-start | bytes 884744 | tf_op jit(solution)/shard_map/ppermute | solution.py:553
  50.4 0.0 copy-start
  50.4 0.0 copy-start.1
  50.4 0.0 copy-start.2
  50.4 0.0 copy-start.3
  50.4 0.0 copy-start.4
  50.4 2.3 %collective-permute-start.9 = (bf16[9,128,128]{2,1,0:T(8,128)(2,1)S(1)}, bf16[9,128,128]{2,1,0:T(8,128)(2,1)S(1)}, u32[]{:S(2)}, u32[]{:S(2)}) collective-permute-start(bf16[9,128,128]{2,1,0:T(8,128)(2,1)S(1)} %get-tuple-element.13), channel_id=1, source_target_pairs={{8,16},{16,8},{9,17},{17,9},{10,18},{18,10},{11,19},{19,11},{12,20... | collective-permute-start | bytes 884744 | tf_op jit(solution)/shard_map/ppermute | solution.py:542
  52.7 2.2 %powers.1.given = f32[9,1,512,128]{3,2,1,0:T(8,128)S(1)} custom-call(s32[32,12]{1,0:T(8,128)S(1)} %bitcast.6, f32[2,128,128]{2,1,0:T(8,128)} %refs_6_.1), custom_call_target="tpu_custom_call" | custom-call | tf_op jit(solution)/shard_map/powers/pallas_call | solution.py:479
  54.9 3.3 %denominators.1 = (f32[5,128,128]{2,1,0:T(8,128)S(1)}, f32[9,1,512,128]{3,2,1,0:T(8,128)S(1)}) custom-call(s32[32,12]{1,0:T(8,128)S(1)} %bitcast.7, f32[2,128,128]{2,1,0:T(8,128)} %refs_6_.1, f32[9,1,512,128]{3,2,1,0:T(8,128)S(1)} %powers.1.given), custom_call_target="tpu_custom_call", output_to_operand_aliasing={{1}: (2, {})} | custom-call | tf_op jit(solution)/shard_map/denominators/pallas_call | solution.py:487
  58.2 0.0 collective-permute-done.10.refs_2_
  58.2 0.4 collective-permute-done.9.refs_1_
  58.6 0.0 copy-done
  58.6 0.0 copy-done.1
  58.6 0.0 copy-done.2
  58.6 0.0 copy-done.3
  58.6 0.0 copy-done.4
  58.6 2.4 %relax.1 = (bf16[4,2,128,128]{3,2,1,0:T(8,128)(2,1)}, f32[2,128,128]{2,1,0:T(8,128)}) custom-call(f32[10,128,128]{2,1,0:T(8,128)S(1)} %get-tuple-element.12.refs_0_, bf16[9,128,128]{2,1,0:T(8,128)(2,1)S(1)} %collective-permute-done.9.refs_1_, bf16[9,128,128]{2,1,0:T(8,128)(2,1)S(1)} %collective-permute-done.10.refs_2_, ...), custom_call_target="tpu_custom_call" | custom-call | tf_op jit(solution)/shard_map/relax/pallas_call | solution.py:557
  (1 shorter events, 0.0 us)
Async XLA Ops:
  1.8 8.2 %collective-permute-start.5 = (bf16[1040,128]{1,0:T(8,128)(2,1)S(1)}, bf16[1040,128]{1,0:T(8,128)(2,1)S(1)}, u32[]{:S(2)}, u32[]{:S(2)}) collective-permute-start(bf16[1040,128]{1,0:T(8,128)(2,1)S(1)} %stage.1.payload.refs_0_), channel_id=1, source_target_pairs={{0,1},{1,0},{2,3},{3,2},{4,5},{5,4},{6,7},{7,6},{8,9},{9,8},{10,11... | collective-permute-start | bytes 798728 | tf_op jit(solution)/shard_map/ppermute | solution.py:409
  3.9 14.1 %collective-permute-start.4 = (bf16[4,2,128,128]{3,2,1,0:T(8,128)(2,1)}, bf16[4,2,128,128]{3,2,1,0:T(8,128)(2,1)}, u32[]{:S(2)}, u32[]{:S(2)}) collective-permute-start(bf16[4,2,128,128]{3,2,1,0:T(8,128)(2,1)} %refs_4_.1), channel_id=1, source_target_pairs={{0,4},{1,5},{2,6},{3,7},{4,0},{5,1},{6,2},{7,3},{8,12},{9,13},{10,... | collective-permute-start | bytes 786440 | tf_op jit(solution)/shard_map/ppermute | solution.py:388
  6.2 32.3 %collective-permute-start.8 = (bf16[1040,128]{1,0:T(8,128)(2,1)S(1)}, bf16[1040,128]{1,0:T(8,128)(2,1)S(1)}, u32[]{:S(2)}, u32[]{:S(2)}) collective-permute-start(bf16[1040,128]{1,0:T(8,128)(2,1)S(1)} %stage.1.payload.refs_0_), channel_id=1, source_target_pairs={{0,2},{1,3},{2,0},{3,1},{4,6},{5,7},{6,4},{7,5},{8,10},{9,11},{10,... | collective-permute-start | bytes 798728 | tf_op jit(solution)/shard_map/ppermute | solution.py:388
  10.0 35.2 %collective-permute-start.6 = (bf16[1040,128]{1,0:T(8,128)(2,1)S(1)}, bf16[1040,128]{1,0:T(8,128)(2,1)S(1)}, u32[]{:S(2)}, u32[]{:S(2)}) collective-permute-start(bf16[1040,128]{1,0:T(8,128)(2,1)S(1)} %collective-permute-done.5.refs_1_), channel_id=1, source_target_pairs={{0,2},{1,3},{2,0},{3,1},{4,6},{5,7},{6,4},{7,5},{8,10},{9,11},{10,... | collective-permute-start | bytes 798728 | tf_op jit(solution)/shard_map/ppermute | solution.py:406
  18.0 27.2 %collective-permute-start.7 = (bf16[4,2,128,128]{3,2,1,0:T(8,128)(2,1)}, bf16[4,2,128,128]{3,2,1,0:T(8,128)(2,1)}, u32[]{:S(2)}, u32[]{:S(2)}) collective-permute-start(bf16[4,2,128,128]{3,2,1,0:T(8,128)(2,1)} %collective-permute-done.4.refs_0_), channel_id=1, source_target_pairs={{0,1},{1,0},{2,3},{3,2},{4,5},{5,4},{6,7},{7,6},{8,9},{9,8},{10,11... | collective-permute-start | bytes 786440 | tf_op jit(solution)/shard_map/ppermute | solution.py:409
  18.2 9.2 %collective-permute-start = (bf16[512,128]{1,0:T(8,128)(2,1)S(1)}, bf16[512,128]{1,0:T(8,128)(2,1)}, u32[]{:S(2)}, u32[]{:S(2)}) collective-permute-start(bf16[512,128]{1,0:T(8,128)(2,1)S(1)} %get-tuple-element.9), channel_id=1, source_target_pairs={{0,6},{1,7},{2,4},{3,5},{4,2},{5,3},{6,0},{7,1},{8,14},{9,15},{10,... | collective-permute-start | bytes 393224 | tf_op jit(solution)/shard_map/ppermute | solution.py:388
  22.4 7.7 %collective-permute-start.2 = (bf16[512,128]{1,0:T(8,128)(2,1)S(1)}, bf16[512,128]{1,0:T(8,128)(2,1)}, u32[]{:S(2)}, u32[]{:S(2)}) collective-permute-start(bf16[512,128]{1,0:T(8,128)(2,1)S(1)} %get-tuple-element.10), channel_id=1, source_target_pairs={{0,6},{1,7},{2,4},{3,5},{4,2},{5,3},{6,0},{7,1},{8,14},{9,15},{10,... | collective-permute-start | bytes 393224 | tf_op jit(solution)/shard_map/ppermute | solution.py:388
  27.3 19.7 %collective-permute-start.1 = (bf16[512,128]{1,0:T(8,128)(2,1)}, bf16[512,128]{1,0:T(8,128)(2,1)}, u32[]{:S(2)}, u32[]{:S(2)}) collective-permute-start(bf16[512,128]{1,0:T(8,128)(2,1)} %collective-permute-done.refs_3_), channel_id=1, source_target_pairs={{0,1},{1,0},{2,3},{3,2},{4,5},{5,4},{6,7},{7,6},{8,9},{9,8},{10,11... | collective-permute-start | bytes 393224 | tf_op jit(solution)/shard_map/ppermute | solution.py:409
  30.2 16.8 %collective-permute-start.3 = (bf16[512,128]{1,0:T(8,128)(2,1)}, bf16[512,128]{1,0:T(8,128)(2,1)}, u32[]{:S(2)}, u32[]{:S(2)}) collective-permute-start(bf16[512,128]{1,0:T(8,128)(2,1)} %collective-permute-done.2.refs_4_), channel_id=1, source_target_pairs={{0,1},{1,0},{2,3},{3,2},{4,5},{5,4},{6,7},{7,6},{8,9},{9,8},{10,11... | collective-permute-start | bytes 393224 | tf_op jit(solution)/shard_map/ppermute | solution.py:409
  32.5 12.7 %all-to-all-start = ((s32[32,1,12]{2,1,0:T(1,128)}), s32[32,1,12]{2,1,0:T(1,128)S(1)}, u32[]{:S(2)}, u32[]{:S(2)}) async-start(s32[32,1,12]{2,1,0:T(1,128)} %broadcast_in_dim.8), calls=%async_computation | async-start | bytes 32768 | tf_op jit(solution)/shard_map/all_to_all | solution.py:468
  49.6 8.6 %collective-permute-start.10 = (bf16[9,128,128]{2,1,0:T(8,128)(2,1)S(1)}, bf16[9,128,128]{2,1,0:T(8,128)(2,1)S(1)}, u32[]{:S(2)}, u32[]{:S(2)}) collective-permute-start(bf16[9,128,128]{2,1,0:T(8,128)(2,1)S(1)} %get-tuple-element.14), channel_id=1, source_target_pairs={{0,8},{16,24},{8,0},{24,16},{1,9},{17,25},{9,1},{25,17},{2,10},{18... | collective-permute-start | bytes 884744 | tf_op jit(solution)/shard_map/ppermute | solution.py:553
  50.4 8.2 %copy-start = (f32[2,128,128]{2,1,0:T(8,128)S(1)}, f32[2,128,128]{2,1,0:T(8,128)}, u32[]{:S(2)}) copy-start(f32[2,128,128]{2,1,0:T(8,128)} %refs_6_.1) | copy-start | bytes 393220
  50.4 8.2 %copy-start.1 = (bf16[4,2,128,128]{3,2,1,0:T(8,128)(2,1)S(1)}, bf16[4,2,128,128]{3,2,1,0:T(8,128)(2,1)}, u32[]{:S(2)}) copy-start(bf16[4,2,128,128]{3,2,1,0:T(8,128)(2,1)} %refs_4_.1) | copy-start | bytes 786436
  50.4 8.2 %copy-start.2 = (bf16[2,256,768]{2,1,0:T(8,128)(2,1)S(1)}, bf16[2,256,768]{2,1,0:T(8,128)(2,1)}, u32[]{:S(2)}) copy-start(bf16[2,256,768]{2,1,0:T(8,128)(2,1)} %constant.5.clone.refs_8_) | copy-start | bytes 2359300
  50.4 8.2 %copy-start.3 = (bf16[2,768,256]{2,1,0:T(8,128)(2,1)S(1)}, bf16[2,768,256]{2,1,0:T(8,128)(2,1)}, u32[]{:S(2)}) copy-start(bf16[2,768,256]{2,1,0:T(8,128)(2,1)} %constant.4.clone.refs_7_) | copy-start | bytes 2359300
  50.4 8.2 %copy-start.4 = (bf16[4,128,128]{2,1,0:T(8,128)(2,1)S(1)}, bf16[4,128,128]{2,1,0:T(8,128)(2,1)}, u32[]{:S(2)}) copy-start(bf16[4,128,128]{2,1,0:T(8,128)(2,1)} %refs_5_.1) | copy-start | bytes 393220
  50.4 8.2 %collective-permute-start.9 = (bf16[9,128,128]{2,1,0:T(8,128)(2,1)S(1)}, bf16[9,128,128]{2,1,0:T(8,128)(2,1)S(1)}, u32[]{:S(2)}, u32[]{:S(2)}) collective-permute-start(bf16[9,128,128]{2,1,0:T(8,128)(2,1)S(1)} %get-tuple-element.13), channel_id=1, source_target_pairs={{8,16},{16,8},{9,17},{17,9},{10,18},{18,10},{11,19},{19,11},{12,20... | collective-permute-start | bytes 884744 | tf_op jit(solution)/shard_map/ppermute | solution.py:542

commit v4 on v3

--- a/solution.py
+++ b/solution.py
@@ -142,7 +142,7 @@
 def place_powers(canvas, meta, probe, area, shift, columns, held, size):
     power = probe[0] * probe[0] + probe[1] * probe[1]
 
-    @pl.loop(0, columns)
+    @pl.loop(0, columns, unroll=4)
     def _(source):
         for number in range(held):
             row, col, tile = where_is(meta, area * columns + source, number)
@@ -195,6 +195,12 @@
     if not whole:
         canvas[...] = given[...]
     place_by_meta(canvas, columns, size, meta, probe, specs, refs[:-2])
+
+
+def band_and_powers_kernel(columns, held, size, specs, meta, probe, *refs):
+    weights = refs[-1]
+    band_kernel(columns, size, True, specs, meta, probe, *refs[:-1])
+    powers_kernel(columns, held, size, meta, probe, weights)
 
 
 def outer_kernel(areas, columns, held, size, whole, specs, meta, *refs):
@@ -476,24 +482,6 @@
     powers = room((columns + 1, 1, 4 * size, size), F32)
     whole = not isinstance(powers, jax.ShapeDtypeStruct)
     far_probe = pltpu.with_memory_space_constraint(probe, pltpu.HBM)
-    weights = pl.pallas_call(
-        functools.partial(powers_kernel, columns, held, size),
-        out_shape=powers,
-        in_specs=[SMEM, VMEM],
-        out_specs=VMEM,
-        compiler_params=limit(*([] if whole else [powers])),
-        name="powers",
-    )(meta, far_probe)
-    share, _ = pl.pallas_call(
-        functools.partial(denominators, areas, columns, held, size, whole),
-        out_shape=(room((held + 1, size, size), F32), powers),
-        in_specs=[SMEM, VMEM, VMEM],
-        out_specs=(VMEM, VMEM),
-        input_output_aliases={2: 1},
-        compiler_params=limit(*([] if whole else [powers, powers])),
-        name="denominators",
-    )(meta, far_probe, *on_chip([weights]))
-
     band = room((columns + 1, 2, 2 * size, size), F32)
     whole = not isinstance(band, jax.ShapeDtypeStruct)
 
@@ -513,16 +501,59 @@
         compiler_params=limit(*extra, *([] if whole else waves)),
         name="band0",
     )(*on_chip(waves))
-    for group in groups:
-        waves = [piece[-1] for piece in group]
-        canvas = pl.pallas_call(
-            functools.partial(band_kernel, columns, size, whole, [piece[:3] for piece in group]),
-            out_shape=band,
-            in_specs=[SMEM] + [VMEM] * (len(waves) + 2),
+    if whole:
+        *groups, final = groups
+        for group in groups:
+            waves = [piece[-1] for piece in group]
+            canvas = pl.pallas_call(
+                functools.partial(band_kernel, columns, size, whole, [piece[:3] for piece in group]),
+                out_shape=band,
+                in_specs=[SMEM] + [VMEM] * (len(waves) + 2),
+                out_specs=VMEM,
+                input_output_aliases={len(waves) + 2: 0},
+                compiler_params=limit(*extra, probe, *([] if whole else waves)),
+            )(meta, far_probe, *on_chip(waves), *on_chip([canvas]))
+        waves = [piece[-1] for piece in final]
+        specs = [piece[:3] for piece in final]
+        count = len(waves) + 2
+        canvas, weights = pl.pallas_call(
+            functools.partial(band_and_powers_kernel, columns, held, size, specs),
+            out_shape=(band, powers),
+            in_specs=[SMEM] + [VMEM] * count,
+            out_specs=(VMEM, VMEM),
+            input_output_aliases={count: 0},
+            compiler_params=limit(probe),
+            name="band_powers",
+        )(meta, far_probe, *on_chip(waves), *on_chip([canvas]))
+    else:
+        for group in groups:
+            waves = [piece[-1] for piece in group]
+            canvas = pl.pallas_call(
+                functools.partial(band_kernel, columns, size, whole, [piece[:3] for piece in group]),
+                out_shape=band,
+                in_specs=[SMEM] + [VMEM] * (len(waves) + 2),
+                out_specs=VMEM,
+                input_output_aliases={len(waves) + 2: 0},
+                compiler_params=limit(*extra, probe, *([] if whole else waves)),
+            )(meta, far_probe, *on_chip(waves), *on_chip([canvas]))
+        weights = pl.pallas_call(
+            functools.partial(powers_kernel, columns, held, size),
+            out_shape=powers,
+            in_specs=[SMEM, VMEM],
             out_specs=VMEM,
-            input_output_aliases={len(waves) + 2: 0},
-            compiler_params=limit(*extra, probe, *([] if whole else waves)),
-        )(meta, far_probe, *on_chip(waves), *on_chip([canvas]))
+            compiler_params=limit(*([] if whole else [powers])),
+            name="powers",
+        )(meta, far_probe)
+    share, _ = pl.pallas_call(
+        functools.partial(denominators, areas, columns, held, size, whole),
+        out_shape=(room((held + 1, size, size), F32), powers),
+        in_specs=[SMEM, VMEM, VMEM],
+        out_specs=(VMEM, VMEM),
+        input_output_aliases={2: 1},
+        compiler_params=limit(*([] if whole else [powers, powers])),
+        name="denominators",
+    )(meta, far_probe, *on_chip([weights]))
+
     message = room((2 * held + 1, size, size), BF16)
     waves = [piece[-1] for piece in late]
     shifted = pltpu.VMEM((2, 3 * size, size), F32)

time: 61.3 us -> 62 us (1.011)
  waiting for transfers between devices: 21.9 us -> 24.9 us
  Pallas kernels: 14.9 us -> 12.7 us
    ppermute x1, waiting for transfers between devices: 0.38 us -> 3.41 us  [body(): outer = lax.ppermute(outer, 'area', pairs + [(b, a) for a, b in pairs])]
    pallas_call x2 -> x1, Pallas kernels: 3.99 us -> 2.65 us  [body(): pl.pallas_call(functools.partial(band_and_powers_kernel, columns, held, s...]
    pallas_call x1, Pallas kernels: 3.31 us -> 2.48 us  [body(): pl.pallas_call(functools.partial(denominators, areas, columns, held, size...]
  transfers between devices with their start and end apart: 12 -> 12, of which waited for: 6 -> 6; matrix products, arithmetic and copies ran while one was open for 2% -> 2% of each run, Pallas kernels for 14% -> 11%
where the time goes in v4:
time: 62 us; the launch traced here: 61.7 us
  waiting for transfers between devices  24.9 us (40%)
  starting transfers between devices  21.7 us (35%)
  Pallas kernels  12.7 us (20%)
  local copies, waits for them, and re-layouts  0.83 us (1%)
  between operations  0.79 us (1%)
  other arithmetic  0.7 us (1%)
    ppermute x4, waiting for transfers between devices, send(): moved = lax.ppermute(value, 'pos', pairs)  13.8 us
    ppermute x4, starting transfers between devices, send(): moved = lax.ppermute(value, 'pos', pairs)  7.91 us
    all_to_all x1, starting transfers between devices, body(): lax.all_to_all(jnp.broadcast_to(mine, (areas * columns, 1, 3 * held)), ('...  6.04 us
    all_to_all x1, waiting for transfers between devices, body(): lax.all_to_all(jnp.broadcast_to(mine, (areas * columns, 1, 3 * held)), ('...  5.16 us
    ppermute x4, starting transfers between devices, gathered(): moved = lax.ppermute(part[2], 'pos', pairs)  3.56 us
    ppermute x1, waiting for transfers between devices, body(): outer = lax.ppermute(outer, 'area', pairs + [(b, a) for a, b in pairs])  3.41 us
    pallas_call x1, Pallas kernels, body(): pl.pallas_call(functools.partial(band_and_powers_kernel, columns, held, s...  2.65 us
    ppermute x4, waiting for transfers between devices, gathered(): moved = lax.ppermute(part[2], 'pos', pairs)  2.5 us
  transfers between devices with their start and end apart: 12, of which 6 were waited for; matrix products, arithmetic and copies ran while one was open for 2% of the time, Pallas kernels for 11%

profile of v4, /device:TPU:1, one launch (start us, length us, event | category | flops | bytes accessed | tf_op | source)
XLA Modules:
  0.0 61.7 jit_solution(6537629521807704341)
XLA Ops:
  0.6 1.1 %stage.1.payload.refs_0_ = bf16[1040,128]{1,0:T(8,128)(2,1)S(1)} custom-call(s32[2,4]{1,0:T(2,128)} %bitcast.7, s32[1,4]{1,0:T(1,128)} %bitcast.8, f32[2,128,128]{2,1,0:T(8,128)} %refs_6_.1, bf16[4,2,128,128]{3,2,1,0:T(8,128)(2,1)} %refs_4_.1), custom_call_target="tpu_custom_call" | custom-call | tf_op jit(solution)/shard_map/stage/pallas_call | solution.py:450
  1.8 2.1 %collective-permute-start.5 = (bf16[1040,128]{1,0:T(8,128)(2,1)S(1)}, bf16[1040,128]{1,0:T(8,128)(2,1)S(1)}, u32[]{:S(2)}, u32[]{:S(2)}) collective-permute-start(bf16[1040,128]{1,0:T(8,128)(2,1)S(1)} %stage.1.payload.refs_0_), channel_id=1, source_target_pairs={{0,1},{1,0},{2,3},{3,2},{4,5},{5,4},{6,7},{7,6},{8,9},{9,8},{10,11... | collective-permute-start | bytes 798728 | tf_op jit(solution)/shard_map/ppermute | solution.py:415
  3.9 2.3 %collective-permute-start.4 = (bf16[4,2,128,128]{3,2,1,0:T(8,128)(2,1)}, bf16[4,2,128,128]{3,2,1,0:T(8,128)(2,1)}, u32[]{:S(2)}, u32[]{:S(2)}) collective-permute-start(bf16[4,2,128,128]{3,2,1,0:T(8,128)(2,1)} %refs_4_.1), channel_id=1, source_target_pairs={{0,4},{1,5},{2,6},{3,7},{4,0},{5,1},{6,2},{7,3},{8,12},{9,13},{10,... | collective-permute-start | bytes 786440 | tf_op jit(solution)/shard_map/ppermute | solution.py:394
  6.2 1.3 %collective-permute-start.8 = (bf16[1040,128]{1,0:T(8,128)(2,1)S(1)}, bf16[1040,128]{1,0:T(8,128)(2,1)S(1)}, u32[]{:S(2)}, u32[]{:S(2)}) collective-permute-start(bf16[1040,128]{1,0:T(8,128)(2,1)S(1)} %stage.1.payload.refs_0_), channel_id=1, source_target_pairs={{0,2},{1,3},{2,0},{3,1},{4,6},{5,7},{6,4},{7,5},{8,10},{9,11},{10,... | collective-permute-start | bytes 798728 | tf_op jit(solution)/shard_map/ppermute | solution.py:394
  7.5 2.5 %collective-permute-done.5.refs_1_ = bf16[1040,128]{1,0:T(8,128)(2,1)S(1)} collective-permute-done((bf16[1040,128]{1,0:T(8,128)(2,1)S(1)}, bf16[1040,128]{1,0:T(8,128)(2,1)S(1)}, u32[]{:S(2)}, u32[]{:S(2)}) %collective-permute-start.5) | collective-permute-done | bytes 266272 | tf_op jit(solution)/shard_map/ppermute | solution.py:415
  10.0 1.4 %collective-permute-start.6 = (bf16[1040,128]{1,0:T(8,128)(2,1)S(1)}, bf16[1040,128]{1,0:T(8,128)(2,1)S(1)}, u32[]{:S(2)}, u32[]{:S(2)}) collective-permute-start(bf16[1040,128]{1,0:T(8,128)(2,1)S(1)} %collective-permute-done.5.refs_1_), channel_id=1, source_target_pairs={{0,2},{1,3},{2,0},{3,1},{4,6},{5,7},{6,4},{7,5},{8,10},{9,11},{10,... | collective-permute-start | bytes 798728 | tf_op jit(solution)/shard_map/ppermute | solution.py:412
  11.4 6.6 %collective-permute-done.4.refs_0_ = bf16[4,2,128,128]{3,2,1,0:T(8,128)(2,1)} collective-permute-done((bf16[4,2,128,128]{3,2,1,0:T(8,128)(2,1)}, bf16[4,2,128,128]{3,2,1,0:T(8,128)(2,1)}, u32[]{:S(2)}, u32[]{:S(2)}) %collective-permute-start.4) | collective-permute-done | bytes 262176 | tf_op jit(solution)/shard_map/ppermute | solution.py:394
  18.0 0.2 collective-permute-start.7
  18.2 4.3 %collective-permute-start = (bf16[512,128]{1,0:T(8,128)(2,1)S(1)}, bf16[512,128]{1,0:T(8,128)(2,1)}, u32[]{:S(2)}, u32[]{:S(2)}) collective-permute-start(bf16[512,128]{1,0:T(8,128)(2,1)S(1)} %get-tuple-element.11), channel_id=1, source_target_pairs={{0,6},{1,7},{2,4},{3,5},{4,2},{5,3},{6,0},{7,1},{8,14},{9,15},{10,... | collective-permute-start | bytes 393224 | tf_op jit(solution)/shard_map/ppermute | solution.py:394
  22.4 0.0 collective-permute-start.2
  22.5 4.9 %collective-permute-done.refs_3_ = bf16[512,128]{1,0:T(8,128)(2,1)} collective-permute-done((bf16[512,128]{1,0:T(8,128)(2,1)S(1)}, bf16[512,128]{1,0:T(8,128)(2,1)}, u32[]{:S(2)}, u32[]{:S(2)}) %collective-permute-start) | collective-permute-done | bytes 131104 | tf_op jit(solution)/shard_map/ppermute | solution.py:394
  27.3 0.5 collective-permute-start.1
  27.8 2.4 %collective-permute-done.2.refs_4_ = bf16[512,128]{1,0:T(8,128)(2,1)} collective-permute-done((bf16[512,128]{1,0:T(8,128)(2,1)S(1)}, bf16[512,128]{1,0:T(8,128)(2,1)}, u32[]{:S(2)}, u32[]{:S(2)}) %collective-permute-start.2) | collective-permute-done | bytes 131104 | tf_op jit(solution)/shard_map/ppermute | solution.py:394
  30.2 0.8 %collective-permute-start.3 = (bf16[512,128]{1,0:T(8,128)(2,1)}, bf16[512,128]{1,0:T(8,128)(2,1)}, u32[]{:S(2)}, u32[]{:S(2)}) collective-permute-start(bf16[512,128]{1,0:T(8,128)(2,1)} %collective-permute-done.2.refs_4_), channel_id=1, source_target_pairs={{0,1},{1,0},{2,3},{3,2},{4,5},{5,4},{6,7},{7,6},{8,9},{9,8},{10,11... | collective-permute-start | bytes 393224 | tf_op jit(solution)/shard_map/ppermute | solution.py:415
  31.0 0.7 %pad_add_fusion = s32[4,3]{0,1:T(4,128)S(1)} fusion(s32[4,1]{0,1:T(1,128)} %param.11, s32[4,2]{0,1:T(2,128)} %param.10), kind=kLoop, calls=%fused_computation | loop fusion | flops 12 | bytes 96 | tf_op jit(solution)/shard_map/concatenate | solution.py:473
  31.7 0.1 copy.13
  31.8 0.1 broadcast_in_dim.7
  31.8 0.6 %broadcast_in_dim.8 = s32[32,1,12]{2,1,0:T(1,128)} broadcast(s32[12]{0:T(128)S(1)} %broadcast_in_dim.7), dimensions={2} | broadcast | bytes 1584 | tf_op jit(solution)/shard_map/broadcast_in_dim | solution.py:475
  32.5 6.0 %all-to-all-start = ((s32[32,1,12]{2,1,0:T(1,128)}), s32[32,1,12]{2,1,0:T(1,128)S(1)}, u32[]{:S(2)}, u32[]{:S(2)}) async-start(s32[32,1,12]{2,1,0:T(1,128)} %broadcast_in_dim.8), calls=%async_computation | async-start | bytes 32768 | tf_op jit(solution)/shard_map/all_to_all | solution.py:474
  38.5 0.0 collective-permute-done.8.refs_2_
  38.5 1.5 %band0.1.refs_5_ = f32[9,2,256,128]{3,2,1,0:T(8,128)S(1)} custom-call(bf16[1040,128]{1,0:T(8,128)(2,1)S(1)} %stage.1.payload.refs_0_, bf16[1040,128]{1,0:T(8,128)(2,1)S(1)} %collective-permute-done.5.refs_1_, bf16[1040,128]{1,0:T(8,128)(2,1)S(1)} %collective-permute-done.8.refs_2_), custom_call_target="tpu_custom_call" | custom-call | tf_op jit(solution)/shard_map/band0/pallas_call | solution.py:491
  40.0 5.2 %all-to-all-done = s32[32,1,12]{2,1,0:T(1,128)S(1)} async-done(((s32[32,1,12]{2,1,0:T(1,128)}), s32[32,1,12]{2,1,0:T(1,128)S(1)}, u32[]{:S(2)}, u32[]{:S(2)}) %all-to-all-start) | async-done | bytes 1568 | tf_op jit(solution)/shard_map/all_to_all | solution.py:474
  45.2 0.0 collective-permute-done.7.refs_2_
  45.2 0.0 collective-permute-done.6.refs_1_
  45.2 2.7 %band_powers.1 = (f32[9,2,256,128]{3,2,1,0:T(8,128)S(1)}, f32[9,1,512,128]{3,2,1,0:T(8,128)S(1)}) custom-call(s32[32,12]{1,0:T(8,128)S(1)} %bitcast.3, f32[2,128,128]{2,1,0:T(8,128)} %refs_6_.1, bf16[4,2,128,128]{3,2,1,0:T(8,128)(2,1)} %collective-permute-done.4.refs_0_, ...), custom_call_target="tpu_custom_call", output_to_operand_aliasing={{0}: (7, {})} | custom-call | tf_op jit(solution)/shard_map/band_powers/pallas_call | solution.py:519
  47.8 0.0 collective-permute-done.1.refs_0_
  47.8 0.0 collective-permute-done.3.refs_1_
  47.8 1.4 %band_outer.1 = (bf16[9,128,128]{2,1,0:T(8,128)(2,1)S(1)}, f32[9,2,256,128]{3,2,1,0:T(8,128)S(1)}) custom-call(s32[32,12]{1,0:T(8,128)S(1)} %bitcast.4, bf16[512,128]{1,0:T(8,128)(2,1)} %collective-permute-done.1.refs_0_, bf16[512,128]{1,0:T(8,128)(2,1)} %collective-permute-done.3.refs_1_, ...), custom_call_target="tpu_custom_call", output_to_operand_aliasing={{1}: (3, {})} | custom-call | tf_op jit(solution)/shard_map/band_outer/pallas_call | solution.py:560
  49.3 0.0 copy-start
  49.3 0.0 copy-start.1
  49.3 0.0 copy-start.2
  49.3 0.0 copy-start.3
  49.3 0.0 copy-start.4
  49.3 1.2 %band_paired.1 = (bf16[9,128,128]{2,1,0:T(8,128)(2,1)S(1)}, f32[10,128,128]{2,1,0:T(8,128)S(1)}) custom-call(s32[32,12]{1,0:T(8,128)S(1)} %bitcast.5, f32[9,2,256,128]{3,2,1,0:T(8,128)S(1)} %get-tuple-element.14.canvas), custom_call_target="tpu_custom_call" | custom-call | tf_op jit(solution)/shard_map/band_paired/pallas_call | solution.py:574
  50.5 0.7 %collective-permute-start.10 = (bf16[9,128,128]{2,1,0:T(8,128)(2,1)S(1)}, bf16[9,128,128]{2,1,0:T(8,128)(2,1)S(1)}, u32[]{:S(2)}, u32[]{:S(2)}) collective-permute-start(bf16[9,128,128]{2,1,0:T(8,128)(2,1)S(1)} %get-tuple-element.17), channel_id=1, source_target_pairs={{0,8},{16,24},{8,0},{24,16},{1,9},{17,25},{9,1},{25,17},{2,10},{18... | collective-permute-start | bytes 884744 | tf_op jit(solution)/shard_map/ppermute | solution.py:584
  51.3 2.1 %collective-permute-start.9 = (bf16[9,128,128]{2,1,0:T(8,128)(2,1)S(1)}, bf16[9,128,128]{2,1,0:T(8,128)(2,1)S(1)}, u32[]{:S(2)}, u32[]{:S(2)}) collective-permute-start(bf16[9,128,128]{2,1,0:T(8,128)(2,1)S(1)} %get-tuple-element.16), channel_id=1, source_target_pairs={{8,16},{16,8},{9,17},{17,9},{10,18},{18,10},{11,19},{19,11},{12,20... | collective-permute-start | bytes 884744 | tf_op jit(solution)/shard_map/ppermute | solution.py:573
  53.4 2.5 %denominators.1 = (f32[5,128,128]{2,1,0:T(8,128)S(1)}, f32[9,1,512,128]{3,2,1,0:T(8,128)S(1)}) custom-call(s32[32,12]{1,0:T(8,128)S(1)} %bitcast.6, f32[2,128,128]{2,1,0:T(8,128)} %refs_6_.1, f32[9,1,512,128]{3,2,1,0:T(8,128)S(1)} %get-tuple-element.18.given), custom_call_target="tpu_custom_call", output_to_operand_aliasing={{1}: (2, {})} | custom-call | tf_op jit(solution)/shard_map/denominators/pallas_call | solution.py:547
  55.9 0.0 collective-permute-done.10.refs_2_
  55.9 3.4 %collective-permute-done.9.refs_1_ = bf16[9,128,128]{2,1,0:T(8,128)(2,1)S(1)} collective-permute-done((bf16[9,128,128]{2,1,0:T(8,128)(2,1)S(1)}, bf16[9,128,128]{2,1,0:T(8,128)(2,1)S(1)}, u32[]{:S(2)}, u32[]{:S(2)}) %collective-permute-start.9) | collective-permute-done | bytes 294944 | tf_op jit(solution)/shard_map/ppermute | solution.py:573
  59.3 0.0 copy-done
  59.3 0.0 copy-done.1
  59.3 0.0 copy-done.2
  59.3 0.0 copy-done.3
  59.3 0.0 copy-done.4
  59.3 2.4 %relax.1 = (bf16[4,2,128,128]{3,2,1,0:T(8,128)(2,1)}, f32[2,128,128]{2,1,0:T(8,128)}) custom-call(f32[10,128,128]{2,1,0:T(8,128)S(1)} %get-tuple-element.15.refs_0_, bf16[9,128,128]{2,1,0:T(8,128)(2,1)S(1)} %collective-permute-done.9.refs_1_, bf16[9,128,128]{2,1,0:T(8,128)(2,1)S(1)} %collective-permute-done.10.refs_2_, ...), custom_call_target="tpu_custom_call" | custom-call | tf_op jit(solution)/shard_map/relax/pallas_call | solution.py:588
  (1 shorter events, 0.0 us)
Async XLA Ops:
  1.8 8.2 %collective-permute-start.5 = (bf16[1040,128]{1,0:T(8,128)(2,1)S(1)}, bf16[1040,128]{1,0:T(8,128)(2,1)S(1)}, u32[]{:S(2)}, u32[]{:S(2)}) collective-permute-start(bf16[1040,128]{1,0:T(8,128)(2,1)S(1)} %stage.1.payload.refs_0_), channel_id=1, source_target_pairs={{0,1},{1,0},{2,3},{3,2},{4,5},{5,4},{6,7},{7,6},{8,9},{9,8},{10,11... | collective-permute-start | bytes 798728 | tf_op jit(solution)/shard_map/ppermute | solution.py:415
  3.9 14.1 %collective-permute-start.4 = (bf16[4,2,128,128]{3,2,1,0:T(8,128)(2,1)}, bf16[4,2,128,128]{3,2,1,0:T(8,128)(2,1)}, u32[]{:S(2)}, u32[]{:S(2)}) collective-permute-start(bf16[4,2,128,128]{3,2,1,0:T(8,128)(2,1)} %refs_4_.1), channel_id=1, source_target_pairs={{0,4},{1,5},{2,6},{3,7},{4,0},{5,1},{6,2},{7,3},{8,12},{9,13},{10,... | collective-permute-start | bytes 786440 | tf_op jit(solution)/shard_map/ppermute | solution.py:394
  6.2 32.3 %collective-permute-start.8 = (bf16[1040,128]{1,0:T(8,128)(2,1)S(1)}, bf16[1040,128]{1,0:T(8,128)(2,1)S(1)}, u32[]{:S(2)}, u32[]{:S(2)}) collective-permute-start(bf16[1040,128]{1,0:T(8,128)(2,1)S(1)} %stage.1.payload.refs_0_), channel_id=1, source_target_pairs={{0,2},{1,3},{2,0},{3,1},{4,6},{5,7},{6,4},{7,5},{8,10},{9,11},{10,... | collective-permute-start | bytes 798728 | tf_op jit(solution)/shard_map/ppermute | solution.py:394
  10.0 35.2 %collective-permute-start.6 = (bf16[1040,128]{1,0:T(8,128)(2,1)S(1)}, bf16[1040,128]{1,0:T(8,128)(2,1)S(1)}, u32[]{:S(2)}, u32[]{:S(2)}) collective-permute-start(bf16[1040,128]{1,0:T(8,128)(2,1)S(1)} %collective-permute-done.5.refs_1_), channel_id=1, source_target_pairs={{0,2},{1,3},{2,0},{3,1},{4,6},{5,7},{6,4},{7,5},{8,10},{9,11},{10,... | collective-permute-start | bytes 798728 | tf_op jit(solution)/shard_map/ppermute | solution.py:412
  18.0 27.2 %collective-permute-start.7 = (bf16[4,2,128,128]{3,2,1,0:T(8,128)(2,1)}, bf16[4,2,128,128]{3,2,1,0:T(8,128)(2,1)}, u32[]{:S(2)}, u32[]{:S(2)}) collective-permute-start(bf16[4,2,128,128]{3,2,1,0:T(8,128)(2,1)} %collective-permute-done.4.refs_0_), channel_id=1, source_target_pairs={{0,1},{1,0},{2,3},{3,2},{4,5},{5,4},{6,7},{7,6},{8,9},{9,8},{10,11... | collective-permute-start | bytes 786440 | tf_op jit(solution)/shard_map/ppermute | solution.py:415
  18.2 9.2 %collective-permute-start = (bf16[512,128]{1,0:T(8,128)(2,1)S(1)}, bf16[512,128]{1,0:T(8,128)(2,1)}, u32[]{:S(2)}, u32[]{:S(2)}) collective-permute-start(bf16[512,128]{1,0:T(8,128)(2,1)S(1)} %get-tuple-element.11), channel_id=1, source_target_pairs={{0,6},{1,7},{2,4},{3,5},{4,2},{5,3},{6,0},{7,1},{8,14},{9,15},{10,... | collective-permute-start | bytes 393224 | tf_op jit(solution)/shard_map/ppermute | solution.py:394
  22.4 7.7 %collective-permute-start.2 = (bf16[512,128]{1,0:T(8,128)(2,1)S(1)}, bf16[512,128]{1,0:T(8,128)(2,1)}, u32[]{:S(2)}, u32[]{:S(2)}) collective-permute-start(bf16[512,128]{1,0:T(8,128)(2,1)S(1)} %get-tuple-element.12), channel_id=1, source_target_pairs={{0,6},{1,7},{2,4},{3,5},{4,2},{5,3},{6,0},{7,1},{8,14},{9,15},{10,... | collective-permute-start | bytes 393224 | tf_op jit(solution)/shard_map/ppermute | solution.py:394
  27.3 20.5 %collective-permute-start.1 = (bf16[512,128]{1,0:T(8,128)(2,1)}, bf16[512,128]{1,0:T(8,128)(2,1)}, u32[]{:S(2)}, u32[]{:S(2)}) collective-permute-start(bf16[512,128]{1,0:T(8,128)(2,1)} %collective-permute-done.refs_3_), channel_id=1, source_target_pairs={{0,1},{1,0},{2,3},{3,2},{4,5},{5,4},{6,7},{7,6},{8,9},{9,8},{10,11... | collective-permute-start | bytes 393224 | tf_op jit(solution)/shard_map/ppermute | solution.py:415
  30.2 17.7 %collective-permute-start.3 = (bf16[512,128]{1,0:T(8,128)(2,1)}, bf16[512,128]{1,0:T(8,128)(2,1)}, u32[]{:S(2)}, u32[]{:S(2)}) collective-permute-start(bf16[512,128]{1,0:T(8,128)(2,1)} %collective-permute-done.2.refs_4_), channel_id=1, source_target_pairs={{0,1},{1,0},{2,3},{3,2},{4,5},{5,4},{6,7},{7,6},{8,9},{9,8},{10,11... | collective-permute-start | bytes 393224 | tf_op jit(solution)/shard_map/ppermute | solution.py:415
  32.5 12.7 %all-to-all-start = ((s32[32,1,12]{2,1,0:T(1,128)}), s32[32,1,12]{2,1,0:T(1,128)S(1)}, u32[]{:S(2)}, u32[]{:S(2)}) async-start(s32[32,1,12]{2,1,0:T(1,128)} %broadcast_in_dim.8), calls=%async_computation | async-start | bytes 32768 | tf_op jit(solution)/shard_map/all_to_all | solution.py:474
  49.3 10.1 %copy-start = (f32[2,128,128]{2,1,0:T(8,128)S(1)}, f32[2,128,128]{2,1,0:T(8,128)}, u32[]{:S(2)}) copy-start(f32[2,128,128]{2,1,0:T(8,128)} %refs_6_.1) | copy-start | bytes 393220
  49.3 10.0 %copy-start.1 = (bf16[4,2,128,128]{3,2,1,0:T(8,128)(2,1)S(1)}, bf16[4,2,128,128]{3,2,1,0:T(8,128)(2,1)}, u32[]{:S(2)}) copy-start(bf16[4,2,128,128]{3,2,1,0:T(8,128)(2,1)} %refs_4_.1) | copy-start | bytes 786436
  49.3 10.0 %copy-start.2 = (bf16[2,768,256]{2,1,0:T(8,128)(2,1)S(1)}, bf16[2,768,256]{2,1,0:T(8,128)(2,1)}, u32[]{:S(2)}) copy-start(bf16[2,768,256]{2,1,0:T(8,128)(2,1)} %constant.4.clone.refs_7_) | copy-start | bytes 2359300
  49.3 10.0 %copy-start.3 = (bf16[2,256,768]{2,1,0:T(8,128)(2,1)S(1)}, bf16[2,256,768]{2,1,0:T(8,128)(2,1)}, u32[]{:S(2)}) copy-start(bf16[2,256,768]{2,1,0:T(8,128)(2,1)} %constant.5.clone.refs_8_) | copy-start | bytes 2359300
  49.3 10.0 %copy-start.4 = (bf16[4,128,128]{2,1,0:T(8,128)(2,1)S(1)}, bf16[4,128,128]{2,1,0:T(8,128)(2,1)}, u32[]{:S(2)}) copy-start(bf16[4,128,128]{2,1,0:T(8,128)(2,1)} %refs_5_.1) | copy-start | bytes 393220
  50.5 5.4 %collective-permute-start.10 = (bf16[9,128,128]{2,1,0:T(8,128)(2,1)S(1)}, bf16[9,128,128]{2,1,0:T(8,128)(2,1)S(1)}, u32[]{:S(2)}, u32[]{:S(2)}) collective-permute-start(bf16[9,128,128]{2,1,0:T(8,128)(2,1)S(1)} %get-tuple-element.17), channel_id=1, source_target_pairs={{0,8},{16,24},{8,0},{24,16},{1,9},{17,25},{9,1},{25,17},{2,10},{18... | collective-permute-start | bytes 884744 | tf_op jit(solution)/shard_map/ppermute | solution.py:584
  51.3 8.0 %collective-permute-start.9 = (bf16[9,128,128]{2,1,0:T(8,128)(2,1)S(1)}, bf16[9,128,128]{2,1,0:T(8,128)(2,1)S(1)}, u32[]{:S(2)}, u32[]{:S(2)}) collective-permute-start(bf16[9,128,128]{2,1,0:T(8,128)(2,1)S(1)} %get-tuple-element.16), channel_id=1, source_target_pairs={{8,16},{16,8},{9,17},{17,9},{10,18},{18,10},{11,19},{19,11},{12,20... | collective-permute-start | bytes 884744 | tf_op jit(solution)/shard_map/ppermute | solution.py:573
